TPU v7x, 256 devices: a whole 4x4x8 slice. The times are simulated.
256 devices in a mesh: narrow: 8 (over y, core), wide: 32 (over x, z).
Axes of the slice: x: 4, y: 4, z: 8, core: 2. Of those that a mesh axis runs over, the one named last changes fastest.
Arguments:
- points: float32 [2, 32768], P(None, ('narrow', 'wide')), may hold values from 0 to 1
- quad_weight: float32 [32768], P(('narrow', 'wide')), may hold values from 9.155274e-06 to 9.1552734e-05
- basis: float32 [4, 2, 32768, 128], P(None, None, ('narrow', 'wide')), may hold values from -6 to 6
- jacobi: float32 [2, 32768], P(None, ('narrow', 'wide')), may hold values from 0.5 to 2
- near_panel: int32 [2048, 12], P(('narrow', 'wide')), may hold values from 0 to 2047, as said below
- near_count: int32 [2048], P(('narrow', 'wide')), may hold values from 2 to 12, as said below
- near_block: bfloat16 [2048, 12, 32, 32], P(('narrow', 'wide')), may hold values from -0.875 to 0.875
- agg_index: int32 [2, 32768], P(None, ('narrow', 'wide')), may hold values from 0 to 47
- coarse_inverse: float32 [8, 1536, 12288], P(None, 'wide', 'narrow'), may hold values from -0.1 to 0.5
Outputs:
- new_block: float32 [2, 32768, 128], P(None, ('narrow', 'wide'))
- hessenberg: float32 [4, 128, 128], replicated
- upper_factor: float32 [128, 128], replicated
Inputs may be any that keep to these rules, and one draw needn't show every extreme that they name: near_panel[p, 0] = p; every entry lies within 4 panels of p in panel order, and some entry lies exactly 4 panels away. `near_count`: slots at or beyond a panel's count are not used; some panel uses all 12.
All inputs are finite; a program needn't handle non-finite values.
Results may differ from a plain program's by a relative error of at most 0.0027.
The roundings to bfloat16 on the way count: a program that leaves them out, or rounds other values in their place, can miss the bound.
Values may be sent and summed in bfloat16 or wider, within the bound.
A program may use at most 64 MiB of HBM per device.

v0:
```python
import math

import jax
import jax.numpy as jnp
from jax import lax
from jax.sharding import PartitionSpec as P

SPAN = 4


NU = 0.3
DELTA2 = 1e-05
ELASTIC = 40.0
HIGH = lax.Precision.HIGHEST


def extended(block, sides, width):
    for axis, dim in sides:
        count = lax.axis_size(axis)
        forward = [(i, i + 1) for i in range(count - 1)]
        backward = [(target, source) for source, target in forward]
        low = lax.ppermute(
            lax.slice_in_dim(block, block.shape[dim] - width, None, axis=dim), axis, forward
        )
        high = lax.ppermute(lax.slice_in_dim(block, 0, width, axis=dim), axis, backward)
        block = jnp.concatenate([low, block, high], axis=dim)
    return block


def far_kernel(targets, sources, weights):
    delta_x = targets[0][:, None] - sources[0][None, :]
    delta_y = targets[1][:, None] - sources[1][None, :]
    square_dist = delta_x * delta_x + delta_y * delta_y + DELTA2
    factor = ELASTIC * weights[None, :]
    log_part = -0.5 * (3.0 - 4.0 * NU) * jnp.log(square_dist)
    g_xx = factor * (log_part + delta_x * delta_x / square_dist)
    g_xy = factor * (delta_x * delta_y / square_dist)
    g_yy = factor * (log_part + delta_y * delta_y / square_dist)
    first_row = jnp.stack([g_xx, g_xy], axis=1)
    second_row = jnp.stack([g_xy, g_yy], axis=1)
    stacked = jnp.stack([first_row, second_row], axis=0)
    return stacked.reshape(2 * targets.shape[1], 2 * sources.shape[1]).astype(jnp.bfloat16)


def far_product(targets, sources, weights, fields):
    piece_len = sources.shape[1]
    row_count = targets.shape[1]
    rhs_count = fields.shape[2]
    block_size = math.gcd(piece_len, max(512, 524288 // row_count))
    block_count = piece_len // block_size

    def one_block(block_index, running):
        offset = block_index * block_size
        source_block = lax.dynamic_slice_in_dim(sources, offset, block_size, 1)
        weight_block = lax.dynamic_slice_in_dim(weights, offset, block_size, 0)
        field_block = lax.dynamic_slice_in_dim(fields, offset, block_size, 1)
        kernel_block = far_kernel(targets, source_block, weight_block)
        return running + jnp.dot(
            kernel_block,
            field_block.reshape(2 * block_size, rhs_count),
            preferred_element_type=jnp.float32,
        )

    initial = jnp.zeros((2 * row_count, rhs_count), jnp.float32)
    return lax.fori_loop(0, block_count, one_block, initial)


def make_fold(targets, source_all, shard_piece):
    return far_product(targets, source_all[0:2], source_all[2], shard_piece)


def body(
    points,
    quad_weight,
    basis,
    jacobi,
    near_panel,
    near_count,
    near_block,
    agg_index,
    coarse_inverse,
):
    block_total = basis.shape[0]
    point_count = basis.shape[2]
    rhs_count = basis.shape[3]
    coarse_count = coarse_inverse.shape[1]
    newest = basis[block_total - 1]
    member = (
        agg_index[:, :, None] == jnp.arange(coarse_count, dtype=jnp.int32)[None, None, :]
    ).astype(jnp.float32)
    coarse_rhs = jnp.einsum("apc,apr->cr", member, newest, precision=HIGH)
    coarse_part = jnp.einsum(
        "abc,cr->abr",
        coarse_inverse,
        lax.all_gather(coarse_rhs, "wide", axis=0, tiled=True),
        precision=HIGH,
    )
    coarse_sol = lax.psum_scatter(coarse_part, "narrow", scatter_dimension=0, tiled=True)[0]
    lifted = jnp.einsum("apc,cr->apr", member, coarse_sol, precision=HIGH)
    precond = (jacobi[:, :, None] * newest + lifted).astype(jnp.bfloat16)
    source_info = jnp.concatenate([points, quad_weight[None, :]], axis=0)
    targets = lax.all_gather(points, "narrow", axis=1, tiled=True)
    source_all = lax.all_gather(source_info, "wide", axis=1, tiled=True)
    far_part = make_fold(targets, source_all, lax.all_gather(precond, "wide", axis=1, tiled=True))
    far_local = lax.psum_scatter(
        far_part.reshape(2, targets.shape[1], rhs_count), "narrow", scatter_dimension=1, tiled=True
    )
    panels_dev = near_panel.shape[0]
    slot_total = near_panel.shape[1]
    nodes = near_block.shape[2] // 2
    padded = extended(precond, ((("narrow", "wide"), 1),), SPAN * nodes)
    panel_fields = padded.reshape(2, panels_dev + 2 * SPAN, nodes, rhs_count)
    local_index = near_panel - lax.axis_index(("narrow", "wide")) * panels_dev + SPAN
    gathered = panel_fields[:, local_index]
    slot_live = jnp.arange(slot_total, dtype=jnp.int32)[None, :] < near_count[:, None]
    gathered = jnp.where(slot_live[None, :, :, None, None], gathered, jnp.zeros((), gathered.dtype))
    gathered = jnp.transpose(gathered, (1, 2, 0, 3, 4)).reshape(
        panels_dev, slot_total, 2 * nodes, rhs_count
    )
    near_terms = jnp.einsum(
        "pkxy,pkyr->pxr", near_block, gathered, preferred_element_type=jnp.float32
    )
    near = jnp.transpose(near_terms.reshape(panels_dev, 2, nodes, rhs_count), (1, 0, 2, 3)).reshape(
        2, point_count, rhs_count
    )
    image = 0.5 * precond.astype(jnp.float32) + far_local + near
    weighted = basis * quad_weight[None, None, :, None]
    local_proj = jnp.einsum("jair,aiw->jrw", weighted, image, precision=HIGH)
    hessenberg = lax.psum(local_proj, ("narrow", "wide"))
    remainder = image - jnp.einsum("jair,jrw->aiw", basis, hessenberg, precision=HIGH)
    local_gram = jnp.einsum(
        "air,aiw->rw", remainder * quad_weight[None, :, None], remainder, precision=HIGH
    )
    gram_matrix = lax.psum(local_gram, ("narrow", "wide"))
    lower_factor = jnp.linalg.cholesky(gram_matrix)
    flat = remainder.reshape(2 * point_count, rhs_count)
    solved = jax.scipy.linalg.solve_triangular(lower_factor, flat.T, lower=True)
    new_block = solved.T.reshape(2, point_count, rhs_count)
    return (new_block, hessenberg, lower_factor.T)


def solution(mesh):
    in_specs = (
        P(None, ("narrow", "wide")),
        P(("narrow", "wide")),
        P(None, None, ("narrow", "wide"), None),
        P(None, ("narrow", "wide")),
        P(("narrow", "wide"), None),
        P(("narrow", "wide")),
        P(("narrow", "wide"), None, None, None),
        P(None, ("narrow", "wide")),
        P(None, "wide", "narrow"),
    )
    out_specs = (P(None, ("narrow", "wide"), None), P(), P())
    return jax.shard_map(body, mesh=mesh, in_specs=in_specs, out_specs=out_specs, check_vma=False)
```

profile of v0, /device:TPU:1, one launch (start us, length us, event | category | flops | bytes accessed | tf_op | source)
XLA Modules:
  0.0 911.1 jit_solution(4539948616988339396)
XLA Ops:
  8.5 42.3 %all_gather.12 = f32[1536,128]{1,0:T(8,128)S(1)} all-gather(f32[48,128]{1,0:T(8,128)S(1)} %convolution_bitcast_fusion.4), channel_id=1, replica_groups=mesh['narrow'=8,'wide'=32] {'wide'}, dimensions={0}, use_global_device_ids=true | all-gather | bytes 811008 | tf_op jit(solution)/shard_map/all_gather | solution.py:95
  53.6 40.3 %reduce-scatter.3.cloned.1.call-done = f32[1,48,128]{2,1,0:T(8,128)} async-done(((f32[8,48,128]{2,1,0:T(8,128)}), f32[1,48,128]{2,1,0:T(8,128)}) %reduce-scatter.3.cloned.1.call-update) | async-done | bytes 24592 | tf_op jit(solution)/shard_map/reduce_scatter | solution.py:98
  95.9 38.2 %all_gather.13 = f32[3,4096]{1,0:T(4,128)S(1)} all-gather(f32[3,128]{1,0:T(4,128)S(1)} %pad_maximum_fusion.2), channel_id=1, replica_groups=mesh['narrow'=8,'wide'=32] {'wide'}, dimensions={1}, use_global_device_ids=true | all-gather | bytes 50688 | tf_op jit(solution)/shard_map/all_gather | solution.py:103
  134.2 22.4 %all_gather.14 = f32[2,1024]{1,0:T(2,128)S(1)} all-gather(f32[2,128]{1,0:T(2,128)S(1)} %copy-done.8), channel_id=1, replica_groups=mesh['narrow'=8,'wide'=32] {'narrow'}, dimensions={1}, use_global_device_ids=true | all-gather | bytes 9216 | tf_op jit(solution)/shard_map/all_gather | solution.py:102
  156.6 14.8 %all-gather.2.cloned.1.call-done = bf16[2,4096,128]{2,1,0:T(8,128)(2,1)} async-done(((bf16[2,128,128]{2,1,0:T(8,128)(2,1)}), bf16[2,4096,128]{2,1,0:T(8,128)(2,1)}) %all-gather.2.cloned.1.call-update) | async-done | bytes 2097168 | tf_op jit(solution)/shard_map/all_gather | solution.py:104
  171.5 163.6 %while.14 = (s32[]{:T(128)}, f32[2048,128]{1,0:T(8,128)}, f32[4096]{0:T(1024)S(1)}, f32[2,1024]{1,0:T(2,128)S(1)}, f32[2,4096]{1,0:T(2,128)S(1)}, /*index=5*/bf1...) while((s32[]{:T(128)}, f32[2048,128]{1,0:T(8,128)}, ...), condition=%wide.region_2.0_spmd.clone, body=%wide.region_1.0_spmd.clone.sunk | while | flops 551551488 | bytes 51161332 | solution.py:65
  174.0 6.3 copy.58
  180.3 5.4 copy.59
  187.4 3.5 convolution_add_fusion.3
  194.4 6.3 copy.58
  200.7 5.4 copy.59
  207.8 3.5 convolution_add_fusion.3
  214.9 6.3 copy.58
  221.2 5.4 copy.59
  228.3 3.5 convolution_add_fusion.3
  235.3 6.3 copy.58
  241.6 5.4 copy.59
  248.7 3.5 convolution_add_fusion.3
  255.8 6.3 copy.58
  262.1 5.4 copy.59
  276.2 6.3 copy.58
  282.5 5.4 copy.59
  296.7 6.3 copy.58
  303.0 5.4 copy.59
  317.1 6.3 copy.58
  323.4 5.4 copy.59
  337.7 8.7 collective-permute-start.1
  352.0 17.6 %reduce-scatter.5.cloned.1.call-done = f32[2,128,128]{2,1,0:T(8,128)} async-done(((f32[2,1024,128]{2,1,0:T(8,128)}), f32[2,128,128]{2,1,0:T(8,128)}) %reduce-scatter.5.cloned.1.call-update) | async-done | bytes 131088 | tf_op jit(solution)/shard_map/reduce_scatter | solution.py:105
  372.6 256.9 %all-reduce.3.cloned.1.call-done = f32[4,128,128]{2,1,0:T(8,128)} async-done(((f32[4,128,128]{2,1,0:T(8,128)}), f32[4,128,128]{2,1,0:T(8,128)}) %all-reduce.3.cloned.1.call-update) | async-done | bytes 262160 | tf_op jit(solution)/shard_map/psum | solution.py:129
  632.2 245.4 %all-reduce.5.cloned.1.call-done = f32[128,128]{0,1:T(8,128)} async-done(((f32[128,128]{0,1:T(8,128)}), f32[128,128]{0,1:T(8,128)}) %all-reduce.5.cloned.1.call-update) | async-done | bytes 65552 | tf_op jit(solution)/shard_map/psum | solution.py:134
  879.4 11.7 %cholesky.16 = f32[128,128]{1,0:T(8,128)S(1)} custom-call(f32[128,128]{1,0:T(8,128)S(1)} %fusion.27), custom_call_target="Cholesky" | custom-call | tf_op jit(solution)/shard_map/jit(cholesky)/cholesky | solution.py:135
  892.4 9.8 %custom-call.7 = f32[1,128,128]{1,2,0:T(8,128)S(1)} custom-call(f32[1,128,128]{2,1,0:T(8,128)S(1)} %get-tuple-element.165), custom_call_target="InvertDiagBlocksLowerTriangular" | custom-call | tf_op jit(solution)/shard_map/jit(_solve_triangular)/triangular_solve | solution.py:137
  (154 shorter events, 80.6 us)
Async XLA Ops:
  7.2 43.7 %copy-start = (f32[8,48,1536]{2,1,0:T(8,128)S(1)}, f32[8,48,1536]{2,1,0:T(8,128)}, u32[]{:S(2)}) copy-start(f32[8,48,1536]{2,1,0:T(8,128)} %param.19) | copy-start | bytes 7077892
  7.2 86.8 %reduce-scatter.3.cloned.1.call-start = ((), (), s32[]{:S(2)}) async-start(), calls=%async_computation.2 | async-start | bytes 221184 | tf_op jit(solution)/shard_map/reduce_scatter | solution.py:98
  8.5 85.5 %copy-start.7 = (s32[2,128]{1,0:T(2,128)S(1)}, s32[2,128]{1,0:T(2,128)}, u32[]{:S(2)}) copy-start(s32[2,128]{1,0:T(2,128)} %param.18) | copy-start | bytes 3076
  8.5 85.5 %copy-start.10 = (f32[2,128]{1,0:T(2,128)S(1)}, f32[2,128]{1,0:T(2,128)}, u32[]{:S(2)}) copy-start(f32[2,128]{1,0:T(2,128)} %param.14) | copy-start | bytes 3076
  50.9 45.1 %copy-start.6 = (f32[128]{0:T(128)S(1)}, f32[128]{0:T(128)}, u32[]{:S(2)}) copy-start(f32[128]{0:T(128)} %param.12) | copy-start | bytes 1540
  50.9 45.1 %copy-start.8 = (f32[2,128]{1,0:T(2,128)S(1)}, f32[2,128]{1,0:T(2,128)}, u32[]{:S(2)}) copy-start(f32[2,128]{1,0:T(2,128)} %param.11) | copy-start | bytes 3076
  53.6 117.9 %all-gather.2.cloned.1.call-start = ((), (), s32[]{:S(2)}) async-start(), calls=%async_computation.3 | async-start | bytes 2162688 | tf_op jit(solution)/shard_map/all_gather | solution.py:104
  95.9 273.8 %reduce-scatter.5.cloned.1.call-start = ((), (), s32[]{:S(2)}) async-start(), calls=%async_computation.4 | async-start | bytes 1179648 | tf_op jit(solution)/shard_map/reduce_scatter | solution.py:105
  171.5 163.7 %copy-start.9 = (s32[8,12]{1,0:T(8,128)S(1)}, s32[8,12]{1,0:T(8,128)}, u32[]{:S(2)}) copy-start(s32[8,12]{1,0:T(8,128)} %param.15) | copy-start | bytes 1156
  171.5 163.8 %copy-start.11 = (s32[8]{0:T(128)S(1)}, s32[8]{0:T(128)}, u32[]{:S(2)}) copy-start(s32[8]{0:T(128)} %param.16) | copy-start | bytes 100
  171.5 163.8 %copy-start.4 = (bf16[2,128,128]{2,1,0:T(8,128)(2,1)S(1)}, bf16[2,128,128]{2,1,0:T(8,128)(2,1)}, u32[]{:S(2)}) copy-start(bf16[2,128,128]{2,1,0:T(8,128)(2,1)} %fusion.16) | copy-start | bytes 196612
  180.3 7.1 copy-start.1
  190.9 1.0 copy-start.2
  200.7 7.1 copy-start.1
  211.4 1.0 copy-start.2
  221.2 7.1 copy-start.1
  231.8 1.0 copy-start.2
  241.6 7.1 copy-start.1
  252.3 1.0 copy-start.2
  262.1 7.1 copy-start.1
  272.7 1.0 copy-start.2
  282.5 7.1 copy-start.1
  303.0 7.1 copy-start.1
  313.6 1.0 copy-start.2
  323.4 7.1 copy-start.1
  334.1 1.0 copy-start.2
  335.1 294.4 %all-reduce.3.cloned.1.call-start = ((), (), s32[]{:S(2)}) async-start(), calls=%async_computation.5 | async-start | bytes 524288 | tf_op jit(solution)/shard_map/psum | solution.py:129
  335.3 11.1 %collective-permute-start = (bf16[2,64,128]{2,1,0:T(8,128)(2,1)S(1)}, bf16[2,64,128]{2,1,0:T(8,128)(2,1)S(1)}, u32[]{:S(2)}, u32[]{:S(2)}) collective-permute-start(bf16[2,64,128]{2,1,0:T(8,128)(2,1)S(1)} %get-tuple-element.166), channel_id=1, source_target_pairs={{0,1},{1,2},{2,3},{3,4},{4,5},{5,6},{6,7},{7,8},{8,9},{9,10},{10,1... | collective-permute-start | bytes 98312 | tf_op jit(solution)/shard_map/ppermute | solution.py:22
  337.7 9.7 %collective-permute-start.1 = (bf16[2,64,128]{2,1,0:T(8,128)(2,1)S(1)}, bf16[2,64,128]{2,1,0:T(8,128)(2,1)S(1)}, u32[]{:S(2)}, u32[]{:S(2)}) collective-permute-start(bf16[2,64,128]{2,1,0:T(8,128)(2,1)S(1)} %get-tuple-element.167), channel_id=1, source_target_pairs={{1,0},{2,1},{3,2},{4,3},{5,4},{6,5},{7,6},{8,7},{9,8},{10,9},{11,1... | collective-permute-start | bytes 98312 | tf_op jit(solution)/shard_map/ppermute | solution.py:25
  349.0 21.5 %copy-start.3 = (f32[4,2,128,128]{3,2,1,0:T(8,128)S(1)}, f32[4,2,128,128]{3,2,1,0:T(8,128)}, u32[]{:S(2)}) copy-start(f32[4,2,128,128]{3,2,1,0:T(8,128)} %param.13) | copy-start | bytes 1572868
  372.4 505.2 %all-reduce.5.cloned.1.call-start = ((), (), s32[]{:S(2)}) async-start(), calls=%async_computation.6 | async-start | bytes 131072 | tf_op jit(solution)/shard_map/psum | solution.py:134
  629.5 274.4 %copy-start.5 = (f32[4,128,128]{2,1,0:T(8,128)S(1)}, f32[4,128,128]{2,1,0:T(8,128)}, u32[]{:S(2)}) copy-start(f32[4,128,128]{2,1,0:T(8,128)} %all-reduce.3.cloned.1.call-done) | copy-start | bytes 786436
  (1 other events, 1.0 us)
Sparse Core Ops, SparseCore 0:
  53.7 40.2 reduce-scatter.2
  97.1 74.2 all-gather.1
  335.2 34.3 reduce-scatter.4
  375.5 253.9 all-reduce.2
  635.4 242.0 all-reduce.4
where the time goes:
time: 912 us; the launch traced here: 911 us
  waiting for transfers between devices  576 us (63%)
  local copies, waits for them, and re-layouts  120 us (13%)
  blocking collectives  103 us (11%)
  other arithmetic  45.4 us (5%)
  matrix products  41.1 us (5%)
  between operations  14 us (2%)
  starting transfers between devices  11.5 us (1%)
    psum x1, waiting for transfers between devices, body(): hessenberg = lax.psum(local_proj, ('narrow', 'wide'))  257 us
    psum x1, waiting for transfers between devices, body(): gram_matrix = lax.psum(local_gram, ('narrow', 'wide'))  245 us
    while x40, local copies, waits for them, and re-layouts  51.2 us
    another operation x8, local copies, waits for them, and re-layouts, far_kernel(): stacked = jnp.stack([first_row, second_row], axis=0)  50.4 us
    all_gather x1, blocking collectives, body(): lax.all_gather(coarse_rhs, 'wide', axis=0, tiled=True)  42.3 us
    reduce_scatter x1, waiting for transfers between devices, body(): lax.psum_scatter(coarse_part, 'narrow', scatter_dimension=0, tiled=True)[0]  40.3 us
    all_gather x1, blocking collectives, body(): source_all = lax.all_gather(source_info, 'wide', axis=1, tiled=True)  38.2 us
    dot_general x8, matrix products, one_block(): jnp.dot(kernel_block, field_block.reshape(2 * block_size, rhs_count), pre...  28.3 us
  transfers between devices with their start and end apart: 7, of which 6 were waited for; matrix products, arithmetic and copies ran while one was open for 1% of the time, Pallas kernels for 0%

commit v1 on v0

--- a/solution.py
+++ b/solution.py
@@ -1,8 +1,11 @@
+import functools
 import math
 
 import jax
 import jax.numpy as jnp
 from jax import lax
+from jax.experimental import pallas as pl
+from jax.experimental.pallas import tpu as pltpu
 from jax.sharding import PartitionSpec as P
 
 SPAN = 4
@@ -67,6 +70,199 @@
 
 def make_fold(targets, source_all, shard_piece):
     return far_product(targets, source_all[0:2], source_all[2], shard_piece)
+
+
+MESH = pl.DeviceIdType.MESH
+NZ = 8
+PANEL = 16
+
+
+def mm(a, b, dims):
+    return lax.dot_general(a, b, (dims, ((), ())), precision=HIGH, preferred_element_type=jnp.float32)
+
+
+def swap(count, me, device, src, dst, sems, go):
+    def one(k, carry):
+        peer = lax.rem(me + k, count)
+        copy = pltpu.make_async_remote_copy(
+            src_ref=src(peer),
+            dst_ref=dst,
+            send_sem=sems.at[0, k],
+            recv_sem=sems.at[1, k],
+            device_id=device(peer),
+            device_id_type=MESH,
+        )
+        if go:
+            copy.start()
+        else:
+            copy.wait()
+        return carry
+
+    lax.fori_loop(1, count, one, 0)
+
+
+def exchange(count, me, device, src, dst, sems):
+    swap(count, me, device, src, dst, sems, True)
+    swap(count, me, device, src, dst, sems, False)
+
+
+def slots_sum(ref, count):
+    total = ref[0]
+    for k in range(1, count):
+        total = total + ref[k]
+    return total
+
+
+def greet(nn, nw, n, w):
+    barrier = pltpu.get_barrier_semaphore()
+
+    def wide_one(k, carry):
+        pl.semaphore_signal(barrier, inc=1, device_id={"wide": lax.rem(w + k, nw)}, device_id_type=MESH)
+        return carry
+
+    def narrow_one(k, carry):
+        pl.semaphore_signal(barrier, inc=1, device_id={"narrow": lax.rem(n + k, nn)}, device_id_type=MESH)
+        return carry
+
+    lax.fori_loop(1, nw, wide_one, 0)
+    lax.fori_loop(1, nn, narrow_one, 0)
+    pl.semaphore_wait(barrier, nw + nn - 2)
+
+
+def factor(gram, work):
+    size = gram.shape[0]
+    rows = lax.broadcasted_iota(jnp.int32, (size, size), 0)
+    cols = lax.broadcasted_iota(jnp.int32, (size, size), 1)
+    work[:, 0:size] = gram
+    work[:, size:] = (rows == cols).astype(jnp.float32)
+    sub = lax.broadcasted_iota(jnp.int32, (PANEL, 1), 0)
+    for base in range(0, size, PANEL):
+        panel = work[base : base + PANEL, :]
+        for k in range(PANEL):
+            pivot = panel[k : k + 1, base + k : base + k + 1]
+            row = panel[k : k + 1, :] * lax.rsqrt(pivot)
+            left = panel[:, base + k : base + k + 1] * lax.rsqrt(pivot)
+            panel = jnp.where(sub == k, row, jnp.where(sub > k, panel - left * row, panel))
+        work[base : base + PANEL, :] = panel
+        if base + PANEL < size:
+            below = mm(panel[:, 0:size], panel, ((0,), (0,)))
+            work[base + PANEL :, :] = work[base + PANEL :, :] - below[base + PANEL :, :]
+
+
+def tail_kernel(
+    nn, nw, nz,
+    weight_ref, basis_ref, image_ref,
+    new_ref, hess_ref, upper_ref,
+    send_h, slots_h, mid_h, slots_n, full_h,
+    send_g, slots_gz, mid_g, slots_gx, mid_g2, slots_gn, mid_g3, full_g,
+    rest, work,
+    sems_w, sems_n, sems_w2, sems_z, sems_x, sems_gn, sems_z2,
+):
+    n = lax.axis_index("narrow")
+    w = lax.axis_index("wide")
+    x, z = w // nz, lax.rem(w, nz)
+    nx = nw // nz
+    blocks, size = basis_ref.shape[0], image_ref.shape[1]
+    points = weight_ref.shape[1]
+    greet(nn, nw, n, w)
+
+    def wide_peer(p):
+        return {"wide": p}
+
+    def narrow_peer(p):
+        return {"narrow": p}
+
+    def z_peer(p):
+        return {"wide": x * nz + p}
+
+    def x_peer(p):
+        return {"wide": p * nz + z}
+
+    spread = jnp.transpose(jnp.broadcast_to(weight_ref[...], (points, points)))
+    scale = jnp.concatenate([spread, spread], axis=0)
+    image = image_ref[...]
+    weighted = image * scale
+    for j in range(blocks):
+        send_h[j * size : (j + 1) * size, :] = mm(basis_ref[j], weighted, ((0,), (0,)))
+    step = blocks * size // nw
+
+    def chunk(ref, p, rows):
+        return ref.at[pl.ds(pl.multiple_of(p * rows, rows), rows), :]
+
+    swap(nw, w, wide_peer, lambda p: chunk(send_h, p, step), slots_h.at[w], sems_w, True)
+    slots_h[w] = send_h[pl.ds(pl.multiple_of(w * step, step), step), :]
+    swap(nw, w, wide_peer, lambda p: chunk(send_h, p, step), slots_h.at[w], sems_w, False)
+    mid_h[...] = slots_sum(slots_h, nw)
+    swap(nn, n, narrow_peer, lambda p: mid_h, slots_n.at[n], sems_n, True)
+    slots_n[n] = mid_h[...]
+    swap(nn, n, narrow_peer, lambda p: mid_h, slots_n.at[n], sems_n, False)
+    mine = slots_sum(slots_n, nn)
+    full_h[pl.ds(pl.multiple_of(w * step, step), step), :] = mine
+    exchange(nw, w, wide_peer, lambda p: chunk(full_h, w, step), chunk(full_h, w, step), sems_w2)
+    remainder = image
+    for j in range(blocks):
+        part = full_h[j * size : (j + 1) * size, :]
+        hess_ref[j] = part
+        remainder = remainder - mm(basis_ref[j], part, ((1,), (0,)))
+    rest[...] = remainder
+    send_g[...] = mm(remainder * scale, remainder, ((0,), (0,)))
+    gstep = size // nz
+    swap(nz, z, z_peer, lambda p: chunk(send_g, p, gstep), slots_gz.at[z], sems_z, True)
+    slots_gz[z] = send_g[pl.ds(pl.multiple_of(z * gstep, gstep), gstep), :]
+    swap(nz, z, z_peer, lambda p: chunk(send_g, p, gstep), slots_gz.at[z], sems_z, False)
+    mid_g[...] = slots_sum(slots_gz, nz)
+    swap(nx, x, x_peer, lambda p: mid_g, slots_gx.at[x], sems_x, True)
+    slots_gx[x] = mid_g[...]
+    swap(nx, x, x_peer, lambda p: mid_g, slots_gx.at[x], sems_x, False)
+    mid_g2[...] = slots_sum(slots_gx, nx)
+    swap(nn, n, narrow_peer, lambda p: mid_g2, slots_gn.at[n], sems_gn, True)
+    slots_gn[n] = mid_g2[...]
+    swap(nn, n, narrow_peer, lambda p: mid_g2, slots_gn.at[n], sems_gn, False)
+    full_g[pl.ds(pl.multiple_of(z * gstep, gstep), gstep), :] = slots_sum(slots_gn, nn)
+    exchange(nz, z, z_peer, lambda p: chunk(full_g, z, gstep), chunk(full_g, z, gstep), sems_z2)
+    factor(full_g[...], work)
+    row = lax.broadcasted_iota(jnp.int32, (size, size), 0)
+    col = lax.broadcasted_iota(jnp.int32, (size, size), 1)
+    upper_ref[...] = jnp.where(row <= col, work[:, 0:size], 0.0)
+    new_ref[...] = mm(rest[...], work[:, size:], ((1,), (1,)))
+
+
+def tail(weight, basis, image, nn, nw, nz):
+    blocks, rows, size = basis.shape
+    f32 = jnp.float32
+    vmem = pl.BlockSpec(memory_space=pltpu.VMEM)
+    step, gstep, nx = blocks * size // nw, size // nz, nw // nz
+    dma = lambda c: pltpu.SemaphoreType.DMA((2, c))
+    return pl.pallas_call(
+        functools.partial(tail_kernel, nn, nw, nz),
+        name="tail",
+        out_shape=(
+            jax.ShapeDtypeStruct((rows, size), f32),
+            jax.ShapeDtypeStruct((blocks, size, size), f32),
+            jax.ShapeDtypeStruct((size, size), f32),
+        ),
+        in_specs=[vmem] * 3,
+        out_specs=(vmem,) * 3,
+        scratch_shapes=[
+            pltpu.VMEM((blocks * size, size), f32),
+            pltpu.VMEM((nw, step, size), f32),
+            pltpu.VMEM((step, size), f32),
+            pltpu.VMEM((nn, step, size), f32),
+            pltpu.VMEM((blocks * size, size), f32),
+            pltpu.VMEM((size, size), f32),
+            pltpu.VMEM((nz, gstep, size), f32),
+            pltpu.VMEM((gstep, size), f32),
+            pltpu.VMEM((nx, gstep, size), f32),
+            pltpu.VMEM((gstep, size), f32),
+            pltpu.VMEM((nn, gstep, size), f32),
+            pltpu.VMEM((gstep, size), f32),
+            pltpu.VMEM((size, size), f32),
+            pltpu.VMEM((rows, size), f32),
+            pltpu.VMEM((size, 2 * size), f32),
+            dma(nw), dma(nn), dma(nw), dma(nz), dma(nx), dma(nn), dma(nz),
+        ],
+        compiler_params=pltpu.CompilerParams(collective_id=0, has_side_effects=True),
+    )(weight, basis, image)
 
 
 def body(
@@ -124,19 +320,15 @@
         2, point_count, rhs_count
     )
     image = 0.5 * precond.astype(jnp.float32) + far_local + near
-    weighted = basis * quad_weight[None, None, :, None]
-    local_proj = jnp.einsum("jair,aiw->jrw", weighted, image, precision=HIGH)
-    hessenberg = lax.psum(local_proj, ("narrow", "wide"))
-    remainder = image - jnp.einsum("jair,jrw->aiw", basis, hessenberg, precision=HIGH)
-    local_gram = jnp.einsum(
-        "air,aiw->rw", remainder * quad_weight[None, :, None], remainder, precision=HIGH
-    )
-    gram_matrix = lax.psum(local_gram, ("narrow", "wide"))
-    lower_factor = jnp.linalg.cholesky(gram_matrix)
-    flat = remainder.reshape(2 * point_count, rhs_count)
-    solved = jax.scipy.linalg.solve_triangular(lower_factor, flat.T, lower=True)
-    new_block = solved.T.reshape(2, point_count, rhs_count)
-    return (new_block, hessenberg, lower_factor.T)
+    new_flat, hessenberg, upper = tail(
+        quad_weight[None, :],
+        basis.reshape(block_total, 2 * point_count, rhs_count),
+        image.reshape(2 * point_count, rhs_count),
+        lax.axis_size("narrow"),
+        lax.axis_size("wide"),
+        NZ,
+    )
+    return (new_flat.reshape(2, point_count, rhs_count), hessenberg, upper)
 
 
 def solution(mesh):

time: 912 us -> 449 us (0.49)
  waiting for transfers between devices: 576 us -> 75.7 us
  Pallas kernels: 0 us -> 66.1 us
  other arithmetic: 45.4 us -> 21.2 us
    psum x2 -> x0, waiting for transfers between devices: 502 us -> none  [the longest x1 257 us: body(): hessenberg = lax.psum(local_proj, ('narrow', 'wide'))]
    pallas_call x0 -> x1, Pallas kernels: none -> 66.1 us  [tail(): pl.pallas_call(functools.partial(tail_kernel, nn, nw, nz), name='tail', o...]
    another operation x12 -> x8, other arithmetic: 34.9 us -> 12.7 us
  transfers between devices with their start and end apart: 7 -> 5, of which waited for: 6 -> 4; matrix products, arithmetic and copies ran while one was open for 1% -> 1% of each run, Pallas kernels for 0% -> 0%
where the time goes in v1:
time: 449 us
  local copies, waits for them, and re-layouts  121 us (27%)
  blocking collectives  103 us (23%)
  waiting for transfers between devices  75.7 us (17%)
  Pallas kernels  66.1 us (15%)
  matrix products  35.7 us (8%)
  other arithmetic  21.2 us (5%)
  between operations  13.9 us (3%)
  starting transfers between devices  11.4 us (3%)
    pallas_call x1, Pallas kernels, tail(): pl.pallas_call(functools.partial(tail_kernel, nn, nw, nz), name='tail', o...  66.1 us
    while x40, local copies, waits for them, and re-layouts  51 us
    another operation x8, local copies, waits for them, and re-layouts, far_kernel(): stacked = jnp.stack([first_row, second_row], axis=0)  50.5 us
    all_gather x1, blocking collectives, body(): lax.all_gather(coarse_rhs, 'wide', axis=0, tiled=True)  42.3 us
    reduce_scatter x1, waiting for transfers between devices, body(): lax.psum_scatter(coarse_part, 'narrow', scatter_dimension=0, tiled=True)[0]  40.3 us
    all_gather x1, blocking collectives, body(): source_all = lax.all_gather(source_info, 'wide', axis=1, tiled=True)  38.2 us
    dot_general x8, matrix products, one_block(): jnp.dot(kernel_block, field_block.reshape(2 * block_size, rhs_count), pre...  28.3 us
    all_gather x1, blocking collectives, body(): targets = lax.all_gather(points, 'narrow', axis=1, tiled=True)  22.4 us
  transfers between devices with their start and end apart: 5, of which 4 were waited for; matrix products, arithmetic and copies ran while one was open for 1% of the time, Pallas kernels for 0%

profile of v1, /device:TPU:1, one launch (start us, length us, event | category | flops | bytes accessed | tf_op | source)
XLA Modules:
  0.0 448.5 jit_solution(12680881077107020053)
XLA Ops:
  8.5 42.3 %all_gather.12 = f32[1536,128]{1,0:T(8,128)S(1)} all-gather(f32[48,128]{1,0:T(8,128)S(1)} %convolution_bitcast_fusion.1), channel_id=1, replica_groups=mesh['narrow'=8,'wide'=32] {'wide'}, dimensions={0}, use_global_device_ids=true | all-gather | bytes 811008 | tf_op jit(solution)/shard_map/all_gather | solution.py:291
  53.6 40.3 %reduce-scatter.3.cloned.1.call-done = f32[1,48,128]{2,1,0:T(8,128)} async-done(((f32[8,48,128]{2,1,0:T(8,128)}), f32[1,48,128]{2,1,0:T(8,128)}) %reduce-scatter.3.cloned.1.call-update) | async-done | bytes 24592 | tf_op jit(solution)/shard_map/reduce_scatter | solution.py:294
  95.9 38.2 %all_gather.13 = f32[3,4096]{1,0:T(4,128)S(1)} all-gather(f32[3,128]{1,0:T(4,128)S(1)} %pad_maximum_fusion.2), channel_id=1, replica_groups=mesh['narrow'=8,'wide'=32] {'wide'}, dimensions={1}, use_global_device_ids=true | all-gather | bytes 50688 | tf_op jit(solution)/shard_map/all_gather | solution.py:299
  134.2 22.4 %all_gather.14 = f32[2,1024]{1,0:T(2,128)S(1)} all-gather(f32[2,128]{1,0:T(2,128)S(1)} %copy-done.5), channel_id=1, replica_groups=mesh['narrow'=8,'wide'=32] {'narrow'}, dimensions={1}, use_global_device_ids=true | all-gather | bytes 9216 | tf_op jit(solution)/shard_map/all_gather | solution.py:298
  156.6 14.8 %all-gather.2.cloned.1.call-done = bf16[2,4096,128]{2,1,0:T(8,128)(2,1)} async-done(((bf16[2,128,128]{2,1,0:T(8,128)(2,1)}), bf16[2,4096,128]{2,1,0:T(8,128)(2,1)}) %all-gather.2.cloned.1.call-update) | async-done | bytes 2097168 | tf_op jit(solution)/shard_map/all_gather | solution.py:300
  171.5 163.6 %while.14 = (s32[]{:T(128)}, f32[2048,128]{1,0:T(8,128)}, f32[4096]{0:T(1024)S(1)}, f32[2,1024]{1,0:T(2,128)S(1)}, f32[2,4096]{1,0:T(2,128)S(1)}, /*index=5*/bf1...) while((s32[]{:T(128)}, f32[2048,128]{1,0:T(8,128)}, ...), condition=%wide.region_2.0_spmd.clone, body=%wide.region_1.0_spmd.clone.sunk | while | flops 551551488 | bytes 51161332 | solution.py:68
  174.0 6.3 %copy.20 = bf16[2,1024,2,512]{3,2,1,0:T(2,128)(2,1)} copy(bf16[2,1024,2,512]{3,1,2,0:T(8,128)(2,1)S(1)} %pad_maximum_fusion.4) | data formatting | bytes 8388608 | tf_op jit(solution)/shard_map/while/body/eval_jaxpr/stack | solution.py:44
  180.3 5.4 %copy.21 = bf16[256,8,2,512]{3,1,2,0:T(8,128)(2,1)} copy(bf16[256,8,2,512]{3,2,1,0:T(2,128)(2,1)} %bitcast.74) | data formatting | bytes 8388608 | tf_op jit(solution)/shard_map/while
  187.4 3.6 convolution_add_fusion.3
  194.5 6.3 %copy.20 = bf16[2,1024,2,512]{3,2,1,0:T(2,128)(2,1)} copy(bf16[2,1024,2,512]{3,1,2,0:T(8,128)(2,1)S(1)} %pad_maximum_fusion.4) | data formatting | bytes 8388608 | tf_op jit(solution)/shard_map/while/body/eval_jaxpr/stack | solution.py:44
  200.8 5.4 %copy.21 = bf16[256,8,2,512]{3,1,2,0:T(8,128)(2,1)} copy(bf16[256,8,2,512]{3,2,1,0:T(2,128)(2,1)} %bitcast.74) | data formatting | bytes 8388608 | tf_op jit(solution)/shard_map/while
  214.9 6.3 %copy.20 = bf16[2,1024,2,512]{3,2,1,0:T(2,128)(2,1)} copy(bf16[2,1024,2,512]{3,1,2,0:T(8,128)(2,1)S(1)} %pad_maximum_fusion.4) | data formatting | bytes 8388608 | tf_op jit(solution)/shard_map/while/body/eval_jaxpr/stack | solution.py:44
  221.2 5.4 %copy.21 = bf16[256,8,2,512]{3,1,2,0:T(8,128)(2,1)} copy(bf16[256,8,2,512]{3,2,1,0:T(2,128)(2,1)} %bitcast.74) | data formatting | bytes 8388608 | tf_op jit(solution)/shard_map/while
  228.3 3.5 convolution_add_fusion.3
  235.3 6.3 %copy.20 = bf16[2,1024,2,512]{3,2,1,0:T(2,128)(2,1)} copy(bf16[2,1024,2,512]{3,1,2,0:T(8,128)(2,1)S(1)} %pad_maximum_fusion.4) | data formatting | bytes 8388608 | tf_op jit(solution)/shard_map/while/body/eval_jaxpr/stack | solution.py:44
  241.7 5.4 %copy.21 = bf16[256,8,2,512]{3,1,2,0:T(8,128)(2,1)} copy(bf16[256,8,2,512]{3,2,1,0:T(2,128)(2,1)} %bitcast.74) | data formatting | bytes 8388608 | tf_op jit(solution)/shard_map/while
  248.7 3.5 convolution_add_fusion.3
  255.8 6.3 %copy.20 = bf16[2,1024,2,512]{3,2,1,0:T(2,128)(2,1)} copy(bf16[2,1024,2,512]{3,1,2,0:T(8,128)(2,1)S(1)} %pad_maximum_fusion.4) | data formatting | bytes 8388608 | tf_op jit(solution)/shard_map/while/body/eval_jaxpr/stack | solution.py:44
  262.1 5.4 %copy.21 = bf16[256,8,2,512]{3,1,2,0:T(8,128)(2,1)} copy(bf16[256,8,2,512]{3,2,1,0:T(2,128)(2,1)} %bitcast.74) | data formatting | bytes 8388608 | tf_op jit(solution)/shard_map/while
  269.2 3.5 convolution_add_fusion.3
  276.2 6.3 %copy.20 = bf16[2,1024,2,512]{3,2,1,0:T(2,128)(2,1)} copy(bf16[2,1024,2,512]{3,1,2,0:T(8,128)(2,1)S(1)} %pad_maximum_fusion.4) | data formatting | bytes 8388608 | tf_op jit(solution)/shard_map/while/body/eval_jaxpr/stack | solution.py:44
  282.6 5.4 %copy.21 = bf16[256,8,2,512]{3,1,2,0:T(8,128)(2,1)} copy(bf16[256,8,2,512]{3,2,1,0:T(2,128)(2,1)} %bitcast.74) | data formatting | bytes 8388608 | tf_op jit(solution)/shard_map/while
  289.6 3.5 convolution_add_fusion.3
  296.7 6.3 %copy.20 = bf16[2,1024,2,512]{3,2,1,0:T(2,128)(2,1)} copy(bf16[2,1024,2,512]{3,1,2,0:T(8,128)(2,1)S(1)} %pad_maximum_fusion.4) | data formatting | bytes 8388608 | tf_op jit(solution)/shard_map/while/body/eval_jaxpr/stack | solution.py:44
  303.0 5.4 %copy.21 = bf16[256,8,2,512]{3,1,2,0:T(8,128)(2,1)} copy(bf16[256,8,2,512]{3,2,1,0:T(2,128)(2,1)} %bitcast.74) | data formatting | bytes 8388608 | tf_op jit(solution)/shard_map/while
  310.1 3.5 convolution_add_fusion.3
  317.1 6.3 %copy.20 = bf16[2,1024,2,512]{3,2,1,0:T(2,128)(2,1)} copy(bf16[2,1024,2,512]{3,1,2,0:T(8,128)(2,1)S(1)} %pad_maximum_fusion.4) | data formatting | bytes 8388608 | tf_op jit(solution)/shard_map/while/body/eval_jaxpr/stack | solution.py:44
  323.4 5.4 %copy.21 = bf16[256,8,2,512]{3,1,2,0:T(8,128)(2,1)} copy(bf16[256,8,2,512]{3,2,1,0:T(2,128)(2,1)} %bitcast.74) | data formatting | bytes 8388608 | tf_op jit(solution)/shard_map/while
  330.5 3.5 convolution_add_fusion.3
  337.6 8.9 %collective-permute-start.1 = (bf16[2,64,128]{2,1,0:T(8,128)(2,1)S(1)}, bf16[2,64,128]{2,1,0:T(8,128)(2,1)S(1)}, u32[]{:S(2)}, u32[]{:S(2)}) collective-permute-start(bf16[2,64,128]{2,1,0:T(8,128)(2,1)S(1)} %get-tuple-element.162), channel_id=1, source_target_pairs={{1,0},{2,1},{3,2},{4,3},{5,4},{6,5},{7,6},{8,7},{9,8},{10,9},{11,1... | collective-permute-start | bytes 98312 | tf_op jit(solution)/shard_map/ppermute | solution.py:28
  349.9 19.7 %reduce-scatter.5.cloned.1.call-done = f32[2,128,128]{2,1,0:T(8,128)} async-done(((f32[2,1024,128]{2,1,0:T(8,128)}), f32[2,128,128]{2,1,0:T(8,128)}) %reduce-scatter.5.cloned.1.call-update) | async-done | bytes 131088 | tf_op jit(solution)/shard_map/reduce_scatter | solution.py:301
  371.2 66.1 %tail.1 = (f32[256,128]{1,0:T(8,128)}, f32[4,128,128]{2,1,0:T(8,128)}, f32[128,128]{1,0:T(8,128)}) custom-call(f32[1,128]{1,0:T(1,128)} %bitcast.89, f32[4,256,128]{2,1,0:T(8,128)} %bitcast.80, f32[256,128]{1,0:T(8,128)} %bitcast.81), custom_call_target="tpu_custom_call" | custom-call | tf_op jit(solution)/shard_map/tail/pallas_call | solution.py:236
  (135 shorter events, 62.8 us)
Async XLA Ops:
  7.2 43.7 %copy-start = (f32[8,48,1536]{2,1,0:T(8,128)S(1)}, f32[8,48,1536]{2,1,0:T(8,128)}, u32[]{:S(2)}) copy-start(f32[8,48,1536]{2,1,0:T(8,128)} %param.19) | copy-start | bytes 7077892
  7.2 86.8 %reduce-scatter.3.cloned.1.call-start = ((), (), s32[]{:S(2)}) async-start(), calls=%async_computation.2 | async-start | bytes 221184 | tf_op jit(solution)/shard_map/reduce_scatter | solution.py:294
  8.5 85.5 %copy-start.4 = (s32[2,128]{1,0:T(2,128)S(1)}, s32[2,128]{1,0:T(2,128)}, u32[]{:S(2)}) copy-start(s32[2,128]{1,0:T(2,128)} %param.18) | copy-start | bytes 3076
  8.5 85.5 %copy-start.8 = (f32[2,128]{1,0:T(2,128)S(1)}, f32[2,128]{1,0:T(2,128)}, u32[]{:S(2)}) copy-start(f32[2,128]{1,0:T(2,128)} %param.14) | copy-start | bytes 3076
  50.9 45.1 %copy-start.5 = (f32[2,128]{1,0:T(2,128)S(1)}, f32[2,128]{1,0:T(2,128)}, u32[]{:S(2)}) copy-start(f32[2,128]{1,0:T(2,128)} %param.11) | copy-start | bytes 3076
  50.9 45.1 %copy-start.7 = (f32[128]{0:T(128)S(1)}, f32[128]{0:T(128)}, u32[]{:S(2)}) copy-start(f32[128]{0:T(128)} %param.12) | copy-start | bytes 1540
  53.6 117.9 %all-gather.2.cloned.1.call-start = ((), (), s32[]{:S(2)}) async-start(), calls=%async_computation.3 | async-start | bytes 2162688 | tf_op jit(solution)/shard_map/all_gather | solution.py:300
  95.9 273.7 %reduce-scatter.5.cloned.1.call-start = ((), (), s32[]{:S(2)}) async-start(), calls=%async_computation.4 | async-start | bytes 1179648 | tf_op jit(solution)/shard_map/reduce_scatter | solution.py:301
  171.5 163.6 %copy-start.6 = (s32[8,12]{1,0:T(8,128)S(1)}, s32[8,12]{1,0:T(8,128)}, u32[]{:S(2)}) copy-start(s32[8,12]{1,0:T(8,128)} %param.15) | copy-start | bytes 1156
  171.5 163.7 %copy-start.9 = (s32[8]{0:T(128)S(1)}, s32[8]{0:T(128)}, u32[]{:S(2)}) copy-start(s32[8]{0:T(128)} %param.16) | copy-start | bytes 100
  171.5 163.8 %copy-start.3 = (bf16[2,128,128]{2,1,0:T(8,128)(2,1)S(1)}, bf16[2,128,128]{2,1,0:T(8,128)(2,1)}, u32[]{:S(2)}) copy-start(bf16[2,128,128]{2,1,0:T(8,128)(2,1)} %fusion.15) | copy-start | bytes 196612
  180.3 7.1 %copy-start.1 = (f32[2048,128]{1,0:T(8,128)S(1)}, f32[2048,128]{1,0:T(8,128)}, u32[]{:S(2)}) copy-start(f32[2048,128]{1,0:T(8,128)} %get-tuple-element.230) | copy-start | bytes 3145732 | tf_op jit(solution)/shard_map/while
  191.0 1.0 copy-start.2
  200.8 7.1 %copy-start.1 = (f32[2048,128]{1,0:T(8,128)S(1)}, f32[2048,128]{1,0:T(8,128)}, u32[]{:S(2)}) copy-start(f32[2048,128]{1,0:T(8,128)} %get-tuple-element.230) | copy-start | bytes 3145732 | tf_op jit(solution)/shard_map/while
  211.4 1.0 copy-start.2
  221.2 7.1 %copy-start.1 = (f32[2048,128]{1,0:T(8,128)S(1)}, f32[2048,128]{1,0:T(8,128)}, u32[]{:S(2)}) copy-start(f32[2048,128]{1,0:T(8,128)} %get-tuple-element.230) | copy-start | bytes 3145732 | tf_op jit(solution)/shard_map/while
  231.8 1.0 copy-start.2
  241.7 7.1 %copy-start.1 = (f32[2048,128]{1,0:T(8,128)S(1)}, f32[2048,128]{1,0:T(8,128)}, u32[]{:S(2)}) copy-start(f32[2048,128]{1,0:T(8,128)} %get-tuple-element.230) | copy-start | bytes 3145732 | tf_op jit(solution)/shard_map/while
  252.3 1.0 copy-start.2
  262.1 7.1 %copy-start.1 = (f32[2048,128]{1,0:T(8,128)S(1)}, f32[2048,128]{1,0:T(8,128)}, u32[]{:S(2)}) copy-start(f32[2048,128]{1,0:T(8,128)} %get-tuple-element.230) | copy-start | bytes 3145732 | tf_op jit(solution)/shard_map/while
  272.7 1.0 copy-start.2
  282.5 7.1 %copy-start.1 = (f32[2048,128]{1,0:T(8,128)S(1)}, f32[2048,128]{1,0:T(8,128)}, u32[]{:S(2)}) copy-start(f32[2048,128]{1,0:T(8,128)} %get-tuple-element.230) | copy-start | bytes 3145732 | tf_op jit(solution)/shard_map/while
  293.2 1.0 copy-start.2
  303.0 7.1 %copy-start.1 = (f32[2048,128]{1,0:T(8,128)S(1)}, f32[2048,128]{1,0:T(8,128)}, u32[]{:S(2)}) copy-start(f32[2048,128]{1,0:T(8,128)} %get-tuple-element.230) | copy-start | bytes 3145732 | tf_op jit(solution)/shard_map/while
  313.6 1.0 copy-start.2
  323.4 7.1 %copy-start.1 = (f32[2048,128]{1,0:T(8,128)S(1)}, f32[2048,128]{1,0:T(8,128)}, u32[]{:S(2)}) copy-start(f32[2048,128]{1,0:T(8,128)} %get-tuple-element.230) | copy-start | bytes 3145732 | tf_op jit(solution)/shard_map/while
  334.1 1.0 copy-start.2
  335.3 11.3 %collective-permute-start = (bf16[2,64,128]{2,1,0:T(8,128)(2,1)S(1)}, bf16[2,64,128]{2,1,0:T(8,128)(2,1)S(1)}, u32[]{:S(2)}, u32[]{:S(2)}) collective-permute-start(bf16[2,64,128]{2,1,0:T(8,128)(2,1)S(1)} %get-tuple-element.161), channel_id=1, source_target_pairs={{0,1},{1,2},{2,3},{3,4},{4,5},{5,6},{6,7},{7,8},{8,9},{9,10},{10,1... | collective-permute-start | bytes 98312 | tf_op jit(solution)/shard_map/ppermute | solution.py:25
  337.6 9.7 %collective-permute-start.1 = (bf16[2,64,128]{2,1,0:T(8,128)(2,1)S(1)}, bf16[2,64,128]{2,1,0:T(8,128)(2,1)S(1)}, u32[]{:S(2)}, u32[]{:S(2)}) collective-permute-start(bf16[2,64,128]{2,1,0:T(8,128)(2,1)S(1)} %get-tuple-element.162), channel_id=1, source_target_pairs={{1,0},{2,1},{3,2},{4,3},{5,4},{6,5},{7,6},{8,7},{9,8},{10,9},{11,1... | collective-permute-start | bytes 98312 | tf_op jit(solution)/shard_map/ppermute | solution.py:28
Sparse Core Ops, SparseCore 0:
  53.7 40.2 reduce-scatter.2
  97.1 74.2 all-gather.1
  335.2 34.3 reduce-scatter.4

commit v2 on v1

v2 whole, which is shorter than its diff:
```python
import functools

import jax
import jax.numpy as jnp
from jax import lax
from jax.experimental import pallas as pl
from jax.experimental.pallas import tpu as pltpu
from jax.sharding import PartitionSpec as P

NU = 0.3
DELTA2 = 1e-05
ELASTIC = 40.0
HIGH = lax.Precision.HIGHEST
MESH = pl.DeviceIdType.MESH
NZ = 8
PANEL = 16
HALF = 64


def mm(a, b, dims):
    return lax.dot_general(a, b, (dims, ((), ())), precision=HIGH, preferred_element_type=jnp.float32)


def swap(count, me, device, src, dst, sems, go):
    def one(k, carry):
        peer = lax.rem(me + k, count)
        copy = pltpu.make_async_remote_copy(
            src_ref=src(peer),
            dst_ref=dst,
            send_sem=sems.at[0, k],
            recv_sem=sems.at[1, k],
            device_id=device(peer),
            device_id_type=MESH,
        )
        if go:
            copy.start()
        else:
            copy.wait()
        return carry

    lax.fori_loop(1, count, one, 0)


def exchange(count, me, device, src, dst, sems):
    swap(count, me, device, src, dst, sems, True)
    swap(count, me, device, src, dst, sems, False)


def ring(count, me, device, block, half, sems, step, go):
    back = step - 1
    for way, peer, origin in ((0, me + 1, me + count - back), (1, me + count - 1, me + back)):
        peer, origin = lax.rem(peer, count), lax.rem(origin, count)
        ref = half(origin, way) if step == count // 2 else block(origin)
        copy = pltpu.make_async_remote_copy(
            src_ref=ref,
            dst_ref=ref,
            send_sem=sems.at[0, way, back],
            recv_sem=sems.at[1, way, back],
            device_id=device(peer),
            device_id_type=MESH,
        )
        if go:
            copy.start()
        else:
            copy.wait()


def slots_sum(ref, count):
    total = ref[0]
    for k in range(1, count):
        total = total + ref[k]
    return total


def greet(nn, nw, n, w, before, after):
    barrier = pltpu.get_barrier_semaphore()

    def wide_one(k, carry):
        pl.semaphore_signal(barrier, inc=1, device_id={"wide": lax.rem(w + k, nw)}, device_id_type=MESH)
        return carry

    def narrow_one(k, carry):
        pl.semaphore_signal(barrier, inc=1, device_id={"narrow": lax.rem(n + k, nn)}, device_id_type=MESH)
        return carry

    lax.fori_loop(1, nw, wide_one, 0)
    lax.fori_loop(1, nn, narrow_one, 0)
    for peer in (before, after):
        pl.semaphore_signal(barrier, inc=1, device_id=peer, device_id_type=MESH)
    pl.semaphore_wait(barrier, nw + nn)


def factor(gram, work):
    size = gram.shape[0]
    rows = lax.broadcasted_iota(jnp.int32, (size, size), 0)
    cols = lax.broadcasted_iota(jnp.int32, (size, size), 1)
    work[:, 0:size] = gram
    work[:, size:] = (rows == cols).astype(jnp.float32)
    sub = lax.broadcasted_iota(jnp.int32, (PANEL, 1), 0)
    for base in range(0, size, PANEL):
        panel = work[base : base + PANEL, :]
        for k in range(PANEL):
            pivot = panel[k : k + 1, base + k : base + k + 1]
            row = panel[k : k + 1, :] * lax.rsqrt(pivot)
            left = panel[:, base + k : base + k + 1] * lax.rsqrt(pivot)
            panel = jnp.where(sub == k, row, jnp.where(sub > k, panel - left * row, panel))
        work[base : base + PANEL, :] = panel
        if base + PANEL < size:
            below = mm(panel[:, 0:size], panel, ((0,), (0,)))
            work[base + PANEL :, :] = work[base + PANEL :, :] - below[base + PANEL :, :]


def column(row, points):
    return jnp.transpose(jnp.broadcast_to(row, (points, points)))


def step_kernel(
    nn, nw, nz,
    panel_ref, count_ref, points_ref, weight_ref, basis_ref, jacobi_ref, agg_ref, block_ref, inverse_ref,
    new_ref, hess_ref, upper_ref,
    info, info_w, info_n, sources, columns, green,
    rhs_all, parts, part_slots, fields_a, fields_b, window, halo, far, far_slots, near,
    send_h, slots_h, mid_h, slots_n, full_h,
    send_g, slots_gz, mid_g, slots_gx, mid_g2, slots_gn, full_g,
    rest, work,
    sems_iw, sems_in, sems_cx, sems_cz, sems_cn, sems_halo,
    sems_ax, sems_az, sems_bz, sems_bx, sems_far,
    sems_w, sems_n, sems_w2, sems_z, sems_x, sems_gn, sems_z2,
):
    f32, bf16 = jnp.float32, jnp.bfloat16
    n = lax.axis_index("narrow")
    w = lax.axis_index("wide")
    x, z = w // nz, lax.rem(w, nz)
    nx = nw // nz
    blocks, size = basis_ref.shape[0], basis_ref.shape[2]
    points = weight_ref.shape[1]
    coarse = inverse_ref.shape[1]
    flat = n * nw + w
    total = nn * nw

    def flat_peer(p):
        return {"narrow": p // nw, "wide": lax.rem(p, nw)}

    before, after = flat_peer(lax.rem(flat + total - 1, total)), flat_peer(lax.rem(flat + 1, total))
    greet(nn, nw, n, w, before, after)

    def wide_peer(p):
        return {"wide": p}

    def narrow_peer(p):
        return {"narrow": p}

    def z_peer(p):
        return {"wide": x * nz + p}

    def x_peer(p):
        return {"wide": p * nz + z}

    info[...] = jnp.zeros_like(info)
    info[0:2, :] = points_ref[...]
    info[2:3, :] = ELASTIC * weight_ref[...]
    swap(nn, n, narrow_peer, lambda p: info, info_n.at[n], sems_in, True)
    swap(nw, w, wide_peer, lambda p: info, info_w.at[w], sems_iw, True)
    info_n[n] = info[...]
    info_w[w] = info[...]

    ids = lax.broadcasted_iota(jnp.int32, (coarse, points), 0)
    member = [(ids == agg_ref[a : a + 1, :]).astype(f32) for a in range(2)]
    newest = [basis_ref[blocks - 1, a * points : (a + 1) * points, :] for a in range(2)]
    rhs_all[x, z] = mm(member[0], newest[0], ((1,), (0,))) + mm(member[1], newest[1], ((1,), (0,)))
    swap(nx, x, x_peer, lambda p: rhs_all.at[x, z], rhs_all.at[x, z], sems_cx, True)

    def rhs_ring(step, go):
        ring(
            nz, z, z_peer,
            lambda p: rhs_all.at[:, p],
            lambda p, way: rhs_all.at[pl.ds(way * (nx // 2), nx // 2), p],
            sems_cz, step, go,
        )

    swap(nx, x, x_peer, lambda p: rhs_all.at[x, z], rhs_all.at[x, z], sems_cx, False)
    rhs_ring(1, True)

    swap(nn, n, narrow_peer, lambda p: info, info_n.at[n], sems_in, False)
    swap(nw, w, wide_peer, lambda p: info, info_w.at[w], sems_iw, False)
    lane = lax.broadcasted_iota(jnp.int32, (8, points), 1)
    pairs = nx // 2
    for p in range(nz):
        for m in range(pairs):
            one, two = info_w[(2 * m) * nz + p], info_w[(2 * m + 1) * nz + p]
            sources[p, m] = jnp.where(lane < HALF, one, pltpu.roll(two, HALF, 1))
    for p in range(nx):
        for h in range(2):
            for m in range(pairs):
                at = p * nz + h * (nz // 2) + 2 * m
                one, two = info_w[at], info_w[at + 1]
                sources[nz + 2 * p + h, m] = jnp.where(lane < HALF, pltpu.roll(one, HALF, 1), two)
    for t in range(nn):
        tile = info_n[t]
        for a in range(2):
            columns[t, a] = column(tile[a : a + 1, :], points)

    chunks = nz + 2 * nx
    tall = 32

    def evaluate(first, last):
        def unit(i, carry):
            c, t = i // nn, lax.rem(i, nn)
            for m in range(pairs):
                src = sources[c, m]
                sx, sy, sw = src[0:1, :], src[1:2, :], src[2:3, :]
                for r in range(0, points, tall):
                    dx = columns[t, 0, r : r + tall, :] - sx
                    dy = columns[t, 1, r : r + tall, :] - sy
                    xx, yy = dx * dx, dy * dy
                    square = xx + yy + DELTA2
                    inv = 1.0 / square
                    log_part = (-0.5 * (3.0 - 4.0 * NU)) * jnp.log(square)
                    rows = pl.ds(pl.multiple_of(t * points + r, tall), tall)
                    cols = slice(m * points, (m + 1) * points)
                    green[c, 0, rows, cols] = (sw * (log_part + xx * inv)).astype(bf16)
                    green[c, 1, rows, cols] = (sw * (dx * dy * inv)).astype(bf16)
                    green[c, 2, rows, cols] = (sw * (log_part + yy * inv)).astype(bf16)
            return carry

        lax.fori_loop(first * nn, last * nn, unit, 0)

    done = 0
    for step in range(1, nz // 2 + 1):
        evaluate(done, done + chunks // 8)
        done += chunks // 8
        rhs_ring(step, False)
        if step < nz // 2:
            rhs_ring(step + 1, True)

    inverse = inverse_ref[...].reshape(nn * coarse, nw * coarse)
    parts[...] = mm(inverse, rhs_all[...].reshape(nw * coarse, size), ((1,), (0,))).reshape(nn, coarse, size)
    swap(nn, n, narrow_peer, lambda p: parts.at[p], part_slots.at[n], sems_cn, True)
    part_slots[n] = parts[n]
    evaluate(done, done + chunks // 4)
    done += chunks // 4
    swap(nn, n, narrow_peer, lambda p: parts.at[p], part_slots.at[n], sems_cn, False)
    sol = slots_sum(part_slots, nn)
    for a in range(2):
        lifted = mm(member[a], sol, ((0,), (0,)))
        field = (column(jacobi_ref[a : a + 1, :], points) * newest[a] + lifted).astype(bf16)
        window[HALF : HALF + points, a * size : (a + 1) * size] = field
    fields_a[z, x] = window[HALF : 2 * HALF, :]
    fields_b[x, z] = window[2 * HALF : 3 * HALF, :]

    lanes = max(nx // 2, 1)

    def a_ring(step, go):
        for j in range(lanes):
            ring(
                nz, z, z_peer,
                lambda p: fields_a.at[p, 2 * j : 2 * j + 2],
                lambda p, way: fields_a.at[p, 2 * j + way],
                sems_az.at[j], step, go,
            )

    def b_ring(step, go):
        ring(
            nz, z, z_peer,
            lambda p: fields_b.at[x, p],
            lambda p, way: fields_b.at[x, p, way * (HALF // 2) : (way + 1) * (HALF // 2)],
            sems_bz, step, go,
        )

    def bx_ring(step, go):
        q = nz // 4
        for j in range(2):
            ring(
                nx, x, x_peer,
                lambda p: fields_b.at[p, 2 * q * j : 2 * q * (j + 1)],
                lambda p, way: fields_b.at[p, 2 * q * j + q * way : 2 * q * j + q * (way + 1)],
                sems_bx.at[j], step, go,
            )

    def halo_copy(way, src, peer, go):
        copy = pltpu.make_async_remote_copy(
            src_ref=src, dst_ref=halo.at[way], send_sem=sems_halo.at[0, way], recv_sem=sems_halo.at[1, way],
            device_id=peer, device_id_type=MESH,
        )
        if go:
            copy.start()
        else:
            copy.wait()

    def halos(go):
        halo_copy(0, fields_b.at[x, z], after, go)
        halo_copy(1, fields_a.at[z, x], before, go)

    def a_first(go):
        swap(nx, x, x_peer, lambda p: fields_a.at[z, x], fields_a.at[z, x], sems_ax, go)

    a_first(True)
    b_ring(1, True)
    halos(True)

    def accumulate(c, field, first):
        left, right = field[:, 0:size], field[:, size:]

        def rows_of(i, carry):
            rows = pl.ds(pl.multiple_of(i * 2 * points, 2 * points), 2 * points)
            cross = jnp.dot(green[c, 1, rows, :], field, preferred_element_type=f32)
            one = jnp.dot(green[c, 0, rows, :], left, preferred_element_type=f32) + cross[:, size:]
            two = jnp.dot(green[c, 2, rows, :], right, preferred_element_type=f32) + cross[:, 0:size]
            if first:
                far[rows, 0:size] = one
                far[rows, size:] = two
            else:
                far[rows, 0:size] = far[rows, 0:size] + one
                far[rows, size:] = far[rows, size:] + two
            return carry

        lax.fori_loop(0, nn // 2, rows_of, 0)

    def take_a(p, first=False):
        p = lax.rem(p, nz)
        accumulate(p, fields_a[p].reshape(nx * HALF, 2 * size), first)

    def take_b(p):
        p = lax.rem(p, nx)
        for h in range(2):
            part = fields_b[p, h * (nz // 2) : (h + 1) * (nz // 2)]
            accumulate(nz + 2 * p + h, part.reshape(nz // 2 * HALF, 2 * size), False)

    evaluate(done, done + 1)
    done += 1
    a_first(False)
    a_ring(1, True)
    b_ring(1, False)
    if nz // 2 > 1:
        b_ring(2, True)
    evaluate(done, chunks)
    take_a(z, True)

    def near_field():
        halos(False)
        window[0:HALF, :] = halo[0]
        window[HALF + points :, :] = halo[1]
        q = block_ref.shape[2] // 2
        panels, slots = block_ref.shape[0], block_ref.shape[1]

        reach = points + 2 * HALF
        row_id = lax.broadcasted_iota(jnp.int32, (q, reach), 0)
        col_id = lax.broadcasted_iota(jnp.int32, (q, reach), 1)

        def one_panel(p, carry):
            live = jnp.full((q, reach), count_ref[p], jnp.int32)
            picks = []
            for k in range(slots):
                start = jnp.full((q, reach), (panel_ref[p, k] - flat * panels) * q + HALF, jnp.int32)
                picks.append(((col_id == start + row_id) & (live > k)).astype(f32))
            pick = jnp.concatenate(picks, axis=0).astype(bf16)
            rows = jnp.dot(pick, window[...], preferred_element_type=f32).astype(bf16)
            total = jnp.zeros((2 * q, size), f32)
            for k in range(slots):
                one = rows[k * q : (k + 1) * q, :]
                both = jnp.concatenate([one[:, 0:size], one[:, size:]], axis=0)
                total = total + jnp.dot(block_ref[p, k], both, preferred_element_type=f32)
            for a in range(2):
                near[pl.ds(pl.multiple_of(a * points + p * q, q), q), :] = total[a * q : (a + 1) * q, :]
            return carry

        lax.fori_loop(0, panels, one_panel, 0)

    for step in range(1, nz // 2 + 1):
        a_ring(step, False)
        if step < nz // 2:
            a_ring(step + 1, True)
            b_ring(step + 1, False)
            if step + 2 <= nz // 2:
                b_ring(step + 2, True)
            else:
                bx_ring(1, True)
        if step == 1:
            near_field()
        take_a(z + nz - step)
        if step < nz // 2:
            take_a(z + step)
    take_b(x)
    for step in range(1, nx // 2 + 1):
        bx_ring(step, False)
        if step < nx // 2:
            bx_ring(step + 1, True)
        take_b(x + nx - step)
        if step < nx // 2:
            take_b(x + step)

    def target(p):
        return far.at[pl.ds(pl.multiple_of(p * points, points), points), :]

    swap(nn, n, narrow_peer, target, far_slots.at[n], sems_far, True)
    far_slots[n] = far[pl.ds(pl.multiple_of(n * points, points), points), :]
    swap(nn, n, narrow_peer, target, far_slots.at[n], sems_far, False)
    far_sum = slots_sum(far_slots, nn)
    image = jnp.concatenate(
        [
            0.5 * window[HALF : HALF + points, a * size : (a + 1) * size].astype(f32)
            + far_sum[:, a * size : (a + 1) * size]
            + near[a * points : (a + 1) * points, :]
            for a in range(2)
        ],
        axis=0,
    )

    spread = column(weight_ref[...], points)
    scale = jnp.concatenate([spread, spread], axis=0)
    weighted = image * scale
    for j in range(blocks):
        send_h[j * size : (j + 1) * size, :] = mm(basis_ref[j], weighted, ((0,), (0,)))
    step = blocks * size // nw

    def chunk(ref, p, rows):
        return ref.at[pl.ds(pl.multiple_of(p * rows, rows), rows), :]

    swap(nw, w, wide_peer, lambda p: chunk(send_h, p, step), slots_h.at[w], sems_w, True)
    slots_h[w] = send_h[pl.ds(pl.multiple_of(w * step, step), step), :]
    swap(nw, w, wide_peer, lambda p: chunk(send_h, p, step), slots_h.at[w], sems_w, False)
    mid_h[...] = slots_sum(slots_h, nw)
    swap(nn, n, narrow_peer, lambda p: mid_h, slots_n.at[n], sems_n, True)
    slots_n[n] = mid_h[...]
    swap(nn, n, narrow_peer, lambda p: mid_h, slots_n.at[n], sems_n, False)
    full_h[pl.ds(pl.multiple_of(w * step, step), step), :] = slots_sum(slots_n, nn)
    exchange(nw, w, wide_peer, lambda p: chunk(full_h, w, step), chunk(full_h, w, step), sems_w2)
    remainder = image
    for j in range(blocks):
        part = full_h[j * size : (j + 1) * size, :]
        hess_ref[j] = part
        remainder = remainder - mm(basis_ref[j], part, ((1,), (0,)))
    rest[...] = remainder
    send_g[...] = mm(remainder * scale, remainder, ((0,), (0,)))
    gstep = size // nz
    swap(nz, z, z_peer, lambda p: chunk(send_g, p, gstep), slots_gz.at[z], sems_z, True)
    slots_gz[z] = send_g[pl.ds(pl.multiple_of(z * gstep, gstep), gstep), :]
    swap(nz, z, z_peer, lambda p: chunk(send_g, p, gstep), slots_gz.at[z], sems_z, False)
    mid_g[...] = slots_sum(slots_gz, nz)
    swap(nx, x, x_peer, lambda p: mid_g, slots_gx.at[x], sems_x, True)
    slots_gx[x] = mid_g[...]
    swap(nx, x, x_peer, lambda p: mid_g, slots_gx.at[x], sems_x, False)
    mid_g2[...] = slots_sum(slots_gx, nx)
    swap(nn, n, narrow_peer, lambda p: mid_g2, slots_gn.at[n], sems_gn, True)
    slots_gn[n] = mid_g2[...]
    swap(nn, n, narrow_peer, lambda p: mid_g2, slots_gn.at[n], sems_gn, False)
    full_g[pl.ds(pl.multiple_of(z * gstep, gstep), gstep), :] = slots_sum(slots_gn, nn)
    exchange(nz, z, z_peer, lambda p: chunk(full_g, z, gstep), chunk(full_g, z, gstep), sems_z2)
    factor(full_g[...], work)
    row = lax.broadcasted_iota(jnp.int32, (size, size), 0)
    col = lax.broadcasted_iota(jnp.int32, (size, size), 1)
    upper_ref[...] = jnp.where(row <= col, work[:, 0:size], 0.0)
    new_ref[...] = mm(rest[...], work[:, size:], ((1,), (1,)))


def whole_step(panel, count, points, weight, basis, jacobi, agg, block, inverse, nn, nw, nz):
    blocks, rows, size = basis.shape
    f32, bf16 = jnp.float32, jnp.bfloat16
    pts = weight.shape[1]
    coarse = inverse.shape[1]
    vmem = pl.BlockSpec(memory_space=pltpu.VMEM)
    smem = pl.BlockSpec(memory_space=pltpu.SMEM)
    step, gstep, nx = blocks * size // nw, size // nz, nw // nz
    chunks, cols = nz + 2 * nx, nx * HALF
    dma = lambda *c: pltpu.SemaphoreType.DMA((2, *c))
    lanes = max(nx // 2, 1)
    buf = pltpu.VMEM
    return pl.pallas_call(
        functools.partial(step_kernel, nn, nw, nz),
        name="step",
        out_shape=(
            jax.ShapeDtypeStruct((rows, size), f32),
            jax.ShapeDtypeStruct((blocks, size, size), f32),
            jax.ShapeDtypeStruct((size, size), f32),
        ),
        in_specs=[smem] * 2 + [vmem] * 7,
        out_specs=(vmem,) * 3,
        scratch_shapes=[
            buf((8, pts), f32),
            buf((nw, 8, pts), f32),
            buf((nn, 8, pts), f32),
            buf((chunks, nx // 2, 8, pts), f32),
            buf((nn, 2, pts, pts), f32),
            buf((chunks, 3, nn * pts, cols), bf16),
            buf((nx, nz, coarse, size), f32),
            buf((nn, coarse, size), f32),
            buf((nn, coarse, size), f32),
            buf((nz, nx, HALF, 2 * size), bf16),
            buf((nx, nz, HALF, 2 * size), bf16),
            buf((pts + 2 * HALF, 2 * size), bf16),
            buf((2, HALF, 2 * size), bf16),
            buf((nn * pts, 2 * size), f32),
            buf((nn, pts, 2 * size), f32),
            buf((rows, size), f32),
            buf((blocks * size, size), f32),
            buf((nw, step, size), f32),
            buf((step, size), f32),
            buf((nn, step, size), f32),
            buf((blocks * size, size), f32),
            buf((size, size), f32),
            buf((nz, gstep, size), f32),
            buf((gstep, size), f32),
            buf((nx, gstep, size), f32),
            buf((gstep, size), f32),
            buf((nn, gstep, size), f32),
            buf((size, size), f32),
            buf((rows, size), f32),
            buf((size, 2 * size), f32),
            dma(nw), dma(nn), dma(nx), dma(2, nz // 2), dma(nn), dma(2),
            dma(nx),
            pltpu.SemaphoreType.DMA((lanes, 2, 2, nz // 2)),
            dma(2, nz // 2),
            pltpu.SemaphoreType.DMA((2, 2, 2, max(nx // 2, 1))),
            dma(nn),
            dma(nw), dma(nn), dma(nw), dma(nz), dma(nx), dma(nn), dma(nz),
        ],
        compiler_params=pltpu.CompilerParams(
            collective_id=0, has_side_effects=True, vmem_limit_bytes=60 * 1024 * 1024
        ),
    )(panel, count, points, weight, basis, jacobi, agg, block, inverse)


def body(
    points, quad_weight, basis, jacobi, near_panel, near_count, near_block, agg_index, coarse_inverse, nz=NZ
):
    block_total, comps, point_count, rhs_count = basis.shape
    new_flat, hessenberg, upper = whole_step(
        near_panel,
        near_count,
        points,
        quad_weight[None, :],
        basis.reshape(block_total, comps * point_count, rhs_count),
        jacobi,
        agg_index,
        near_block,
        coarse_inverse,
        lax.axis_size("narrow"),
        lax.axis_size("wide"),
        nz,
    )
    return (new_flat.reshape(comps, point_count, rhs_count), hessenberg, upper)


def solution(mesh):
    in_specs = (
        P(None, ("narrow", "wide")),
        P(("narrow", "wide")),
        P(None, None, ("narrow", "wide"), None),
        P(None, ("narrow", "wide")),
        P(("narrow", "wide"), None),
        P(("narrow", "wide")),
        P(("narrow", "wide"), None, None, None),
        P(None, ("narrow", "wide")),
        P(None, "wide", "narrow"),
    )
    out_specs = (P(None, ("narrow", "wide"), None), P(), P())
    return jax.shard_map(body, mesh=mesh, in_specs=in_specs, out_specs=out_specs, check_vma=False)
```

time: 449 us -> 149 us (0.33)
  local copies, waits for them, and re-layouts: 121 us -> 4.71 us
  blocking collectives: 103 us -> 0 us
  Pallas kernels: 66.1 us -> 144 us
  waiting for transfers between devices: 75.7 us -> 0 us
  matrix products: 35.7 us -> 0 us
  other arithmetic: 21.2 us -> 0 us
  between operations: 13.9 us -> 0.64 us
  starting transfers between devices: 11.4 us -> 0 us
    all_gather x3 -> x0, blocking collectives: 103 us -> none  [the longest x1 42.3 us: body(): lax.all_gather(coarse_rhs, 'wide', axis=0, tiled=True)]
    pallas_call x1, Pallas kernels: 66.1 us -> 144 us  [whole_step(): pl.pallas_call(functools.partial(step_kernel, nn, nw, nz), name='step', o...]
    reduce_scatter x2 -> x0, waiting for transfers between devices: 60 us -> none  [the longest x1 40.3 us: body(): lax.psum_scatter(coarse_part, 'narrow', scatter_dimension=0, tiled=True)[0]]
    while x40 -> x0, local copies, waits for them, and re-layouts: 51 us -> none
    another operation x8 -> x0, local copies, waits for them, and re-layouts: 50.5 us -> none  [far_kernel(): stacked = jnp.stack([first_row, second_row], axis=0)]
    dot_general x12 -> x0, matrix products: 35.7 us -> none  [the longest x8 28.3 us: one_block(): jnp.dot(kernel_block, field_block.reshape(2 * block_size, rhs_count), pre...]
    another operation x24 -> x0, other arithmetic: 18.7 us -> none
    all_gather x1 -> x0, waiting for transfers between devices: 14.8 us -> none  [body(): lax.all_gather(precond, 'wide', axis=1, tiled=True)]
  transfers between devices with their start and end apart: 5 -> 0, of which waited for: 4 -> 0; matrix products, arithmetic and copies ran while one was open for 1% -> 0% of each run, Pallas kernels for 0% -> 0%
where the time goes in v2:
time: 149 us
  Pallas kernels  144 us (97%)
  local copies, waits for them, and re-layouts  4.71 us (3%)
    pallas_call x1, Pallas kernels, whole_step(): pl.pallas_call(functools.partial(step_kernel, nn, nw, nz), name='step', o...  144 us
    unnamed x3, local copies, waits for them, and re-layouts  4.71 us

profile of v2, /device:TPU:1, one launch (start us, length us, event | category | flops | bytes accessed | tf_op | source)
XLA Modules:
  0.0 149.3 jit_solution(16716356718469075933)
XLA Ops:
  0.6 143.9 %step.1 = (f32[256,128]{1,0:T(8,128)}, f32[4,128,128]{2,1,0:T(8,128)}, f32[128,128]{1,0:T(8,128)}) custom-call(s32[8,12]{1,0:T(8,128)} %panel_ref.1, s32[8]{0:T(128)} %count_ref.1, f32[2,128]{1,0:T(2,128)} %points_ref.1, f32[1,128]{1,0:T(1,128)} %bitcast.5, f32[4,256,128]{2,1,0:T(8,128)} %bitcast.3, f32[2,128]{1,0:T(2,128)} %jacobi_ref.1, s32[2,128]{1,0:T(2,128)} %agg_ref.1, ...), custom_call_target="tpu_custom_call" | custom-call | tf_op jit(solution)/shard_map/step/pallas_call | solution.py:468
  144.5 1.6 %copy.15 = f32[2,128,128]{2,1,0:T(8,128)} copy(f32[2,128,128]{2,1,0:T(8,128)} %bitcast.4) | data formatting | bytes 262144
  146.1 1.7 %copy.16 = f32[4,128,128]{2,1,0:T(8,128)} copy(f32[4,128,128]{2,1,0:T(8,128)} %get-tuple-element.13) | data formatting | bytes 524288
  147.8 1.5 copy.17

commit v3 on v2

--- a/solution.py
+++ b/solution.py
@@ -87,7 +87,7 @@
     lax.fori_loop(1, nn, narrow_one, 0)
     for peer in (before, after):
         pl.semaphore_signal(barrier, inc=1, device_id=peer, device_id_type=MESH)
-    pl.semaphore_wait(barrier, nw + nn)
+    return barrier
 
 
 def factor(gram, work):
@@ -116,14 +116,16 @@
 
 def step_kernel(
     nn, nw, nz,
-    panel_ref, count_ref, points_ref, weight_ref, basis_ref, jacobi_ref, agg_ref, block_ref, inverse_ref,
-    new_ref, hess_ref, upper_ref,
+    panel_ref, count_ref, points_ref, weight_ref, basis_hbm, jacobi_ref, agg_ref, block_hbm, inverse_hbm,
+    rest_ref, hess_ref, gram_ref,
+    basis_ref, block_ref, inverse_ref,
     info, info_w, info_n, sources, columns, green,
-    rhs_all, parts, part_slots, fields_a, fields_b, window, halo, far, far_slots, near,
+    rhs_a, rhs_b, rhs_all, parts, part_slots, fields_a, fields_b, window, halo, far, far_slots, near,
     send_h, slots_h, mid_h, slots_n, full_h,
     send_g, slots_gz, mid_g, slots_gx, mid_g2, slots_gn, full_g,
-    rest, work,
-    sems_iw, sems_in, sems_cx, sems_cz, sems_cn, sems_halo,
+    rest,
+    sems_io, sems_iw, sems_in, sems_cn, sems_halo,
+    sems_cax, sems_caz, sems_cbz, sems_cbx,
     sems_ax, sems_az, sems_bz, sems_bx, sems_far,
     sems_w, sems_n, sems_w2, sems_z, sems_x, sems_gn, sems_z2,
 ):
@@ -142,7 +144,13 @@
         return {"narrow": p // nw, "wide": lax.rem(p, nw)}
 
     before, after = flat_peer(lax.rem(flat + total - 1, total)), flat_peer(lax.rem(flat + 1, total))
-    greet(nn, nw, n, w, before, after)
+    barrier = greet(nn, nw, n, w, before, after)
+    loads = [
+        pltpu.make_async_copy(src, dst, sems_io.at[i])
+        for i, (src, dst) in enumerate(((basis_hbm, basis_ref), (inverse_hbm, inverse_ref), (block_hbm, block_ref)))
+    ]
+    for load in loads:
+        load.start()
 
     def wide_peer(p):
         return {"wide": p}
@@ -155,53 +163,124 @@
 
     def x_peer(p):
         return {"wide": p * nz + z}
+
+    lanes = max(nx // 2, 1)
+
+    def gathering(buf_a, buf_b, cut, sem_ax, sem_az, sem_bz, sem_bx):
+        def a_first(go):
+            swap(nx, x, x_peer, lambda p: buf_a.at[z, x], buf_a.at[z, x], sem_ax, go)
+
+        def a_ring(j, step, go):
+            ring(
+                nz, z, z_peer,
+                lambda p: buf_a.at[p, 2 * j : 2 * j + 2],
+                lambda p, way: buf_a.at[p, 2 * j + way],
+                sem_az.at[j], step, go,
+            )
+
+        def part(ref, way):
+            return ref.at[:cut] if way == 0 else ref.at[cut:]
+
+        def b_ring(step, go):
+            ring(
+                nz, z, z_peer,
+                lambda p: buf_b.at[x, p],
+                lambda p, way: part(buf_b.at[x, p], way),
+                sem_bz, step, go,
+            )
+
+        def bx_ring(shift, step, go):
+            for at, sign in ((2 * shift - 1, -1), (2 * shift, 1)):
+                if at < 0 or at >= nz:
+                    continue
+                q = lax.rem(z + nz + sign * shift, nz)
+                ring(
+                    nx, x, x_peer,
+                    lambda p: buf_b.at[p, q],
+                    lambda p, way: part(buf_b.at[p, q], way),
+                    sem_bx.at[at], step, go,
+                )
+
+        return a_first, a_ring, b_ring, bx_ring
+
+    def run_gather(steps, opened, own, arrived, crossed):
+        a_first, a_ring, b_ring, bx_ring = steps
+        deep, wide_steps = nz // 2, nx // 2
+
+        def next_b(step):
+            b_ring(step, False)
+            if step < deep:
+                b_ring(step + 1, True)
+            bx_ring(step, 1, True)
+
+        def next_x(shift):
+            bx_ring(shift, 1, False)
+            if wide_steps > 1:
+                bx_ring(shift, 2, True)
+
+        a_first(True)
+        b_ring(1, True)
+        bx_ring(0, 1, True)
+        opened()
+        a_first(False)
+        for j in range(lanes):
+            a_ring(j, 1, True)
+        next_b(1)
+        next_x(0)
+        own()
+        for step in range(1, deep + 1):
+            if step < deep:
+                next_b(step + 1)
+            next_x(step)
+            for j in range(lanes):
+                a_ring(j, step, False)
+                if step < deep:
+                    a_ring(j, step + 1, True)
+            arrived(step)
+        crossed(1)
+        if wide_steps > 1:
+            for shift in range(deep + 1):
+                bx_ring(shift, 2, False)
+            crossed(2)
 
     info[...] = jnp.zeros_like(info)
     info[0:2, :] = points_ref[...]
     info[2:3, :] = ELASTIC * weight_ref[...]
+    info_n[n] = info[...]
+    info_w[w] = info[...]
+
+    ids = lax.broadcasted_iota(jnp.int32, (coarse, points), 0)
+    member = [(ids == agg_ref[a : a + 1, :]).astype(f32) for a in range(2)]
+    loads[0].wait()
+    newest = [basis_ref[blocks - 1, a * points : (a + 1) * points, :] for a in range(2)]
+    rhs = mm(member[0], newest[0], ((1,), (0,))) + mm(member[1], newest[1], ((1,), (0,)))
+    rhs_a[z, x] = rhs[0 : coarse // 2, :]
+    rhs_b[x, z] = rhs[coarse // 2 :, :]
+    pl.semaphore_wait(barrier, nw + nn)
     swap(nn, n, narrow_peer, lambda p: info, info_n.at[n], sems_in, True)
     swap(nw, w, wide_peer, lambda p: info, info_w.at[w], sems_iw, True)
-    info_n[n] = info[...]
-    info_w[w] = info[...]
-
-    ids = lax.broadcasted_iota(jnp.int32, (coarse, points), 0)
-    member = [(ids == agg_ref[a : a + 1, :]).astype(f32) for a in range(2)]
-    newest = [basis_ref[blocks - 1, a * points : (a + 1) * points, :] for a in range(2)]
-    rhs_all[x, z] = mm(member[0], newest[0], ((1,), (0,))) + mm(member[1], newest[1], ((1,), (0,)))
-    swap(nx, x, x_peer, lambda p: rhs_all.at[x, z], rhs_all.at[x, z], sems_cx, True)
-
-    def rhs_ring(step, go):
-        ring(
-            nz, z, z_peer,
-            lambda p: rhs_all.at[:, p],
-            lambda p, way: rhs_all.at[pl.ds(way * (nx // 2), nx // 2), p],
-            sems_cz, step, go,
-        )
-
-    swap(nx, x, x_peer, lambda p: rhs_all.at[x, z], rhs_all.at[x, z], sems_cx, False)
-    rhs_ring(1, True)
-
-    swap(nn, n, narrow_peer, lambda p: info, info_n.at[n], sems_in, False)
-    swap(nw, w, wide_peer, lambda p: info, info_w.at[w], sems_iw, False)
-    lane = lax.broadcasted_iota(jnp.int32, (8, points), 1)
-    pairs = nx // 2
-    for p in range(nz):
-        for m in range(pairs):
-            one, two = info_w[(2 * m) * nz + p], info_w[(2 * m + 1) * nz + p]
-            sources[p, m] = jnp.where(lane < HALF, one, pltpu.roll(two, HALF, 1))
-    for p in range(nx):
-        for h in range(2):
-            for m in range(pairs):
-                at = p * nz + h * (nz // 2) + 2 * m
-                one, two = info_w[at], info_w[at + 1]
-                sources[nz + 2 * p + h, m] = jnp.where(lane < HALF, pltpu.roll(one, HALF, 1), two)
-    for t in range(nn):
-        tile = info_n[t]
-        for a in range(2):
-            columns[t, a] = column(tile[a : a + 1, :], points)
-
     chunks = nz + 2 * nx
     tall = 32
+    pairs = nx // 2
+
+    def prepare():
+        swap(nn, n, narrow_peer, lambda p: info, info_n.at[n], sems_in, False)
+        swap(nw, w, wide_peer, lambda p: info, info_w.at[w], sems_iw, False)
+        lane = lax.broadcasted_iota(jnp.int32, (8, points), 1)
+        for p in range(nz):
+            for m in range(pairs):
+                one, two = info_w[(2 * m) * nz + p], info_w[(2 * m + 1) * nz + p]
+                sources[p, m] = jnp.where(lane < HALF, one, pltpu.roll(two, HALF, 1))
+        for p in range(nx):
+            for h in range(2):
+                for m in range(pairs):
+                    at = p * nz + h * (nz // 2) + 2 * m
+                    one, two = info_w[at], info_w[at + 1]
+                    sources[nz + 2 * p + h, m] = jnp.where(lane < HALF, pltpu.roll(one, HALF, 1), two)
+        for t in range(nn):
+            tile = info_n[t]
+            for a in range(2):
+                columns[t, a] = column(tile[a : a + 1, :], points)
 
     def evaluate(first, last):
         def unit(i, carry):
@@ -223,22 +302,30 @@
                     green[c, 2, rows, cols] = (sw * (log_part + yy * inv)).astype(bf16)
             return carry
 
-        lax.fori_loop(first * nn, last * nn, unit, 0)
-
-    done = 0
-    for step in range(1, nz // 2 + 1):
-        evaluate(done, done + chunks // 8)
-        done += chunks // 8
-        rhs_ring(step, False)
-        if step < nz // 2:
-            rhs_ring(step + 1, True)
+        lax.fori_loop(first, last, unit, 0)
+
+    done = [0]
+
+    def fill(share):
+        last = min(done[0] + share * chunks * nn // 128, chunks * nn)
+        evaluate(done[0], last)
+        done[0] = last
+
+    run_gather(
+        gathering(rhs_a, rhs_b, 16, sems_cax, sems_caz, sems_cbz, sems_cbx),
+        lambda: None, prepare, lambda step: fill(16), lambda step: None,
+    )
+    for p in range(nx):
+        for q in range(nz):
+            rhs_all[p, q, 0 : coarse // 2, :] = rhs_a[q, p]
+            rhs_all[p, q, coarse // 2 :, :] = rhs_b[p, q]
+    loads[1].wait()
 
     inverse = inverse_ref[...].reshape(nn * coarse, nw * coarse)
     parts[...] = mm(inverse, rhs_all[...].reshape(nw * coarse, size), ((1,), (0,))).reshape(nn, coarse, size)
     swap(nn, n, narrow_peer, lambda p: parts.at[p], part_slots.at[n], sems_cn, True)
     part_slots[n] = parts[n]
-    evaluate(done, done + chunks // 4)
-    done += chunks // 4
+    fill(32)
     swap(nn, n, narrow_peer, lambda p: parts.at[p], part_slots.at[n], sems_cn, False)
     sol = slots_sum(part_slots, nn)
     for a in range(2):
@@ -247,35 +334,6 @@
         window[HALF : HALF + points, a * size : (a + 1) * size] = field
     fields_a[z, x] = window[HALF : 2 * HALF, :]
     fields_b[x, z] = window[2 * HALF : 3 * HALF, :]
-
-    lanes = max(nx // 2, 1)
-
-    def a_ring(step, go):
-        for j in range(lanes):
-            ring(
-                nz, z, z_peer,
-                lambda p: fields_a.at[p, 2 * j : 2 * j + 2],
-                lambda p, way: fields_a.at[p, 2 * j + way],
-                sems_az.at[j], step, go,
-            )
-
-    def b_ring(step, go):
-        ring(
-            nz, z, z_peer,
-            lambda p: fields_b.at[x, p],
-            lambda p, way: fields_b.at[x, p, way * (HALF // 2) : (way + 1) * (HALF // 2)],
-            sems_bz, step, go,
-        )
-
-    def bx_ring(step, go):
-        q = nz // 4
-        for j in range(2):
-            ring(
-                nx, x, x_peer,
-                lambda p: fields_b.at[p, 2 * q * j : 2 * q * (j + 1)],
-                lambda p, way: fields_b.at[p, 2 * q * j + q * way : 2 * q * j + q * (way + 1)],
-                sems_bx.at[j], step, go,
-            )
 
     def halo_copy(way, src, peer, go):
         copy = pltpu.make_async_remote_copy(
@@ -290,13 +348,6 @@
     def halos(go):
         halo_copy(0, fields_b.at[x, z], after, go)
         halo_copy(1, fields_a.at[z, x], before, go)
-
-    def a_first(go):
-        swap(nx, x, x_peer, lambda p: fields_a.at[z, x], fields_a.at[z, x], sems_ax, go)
-
-    a_first(True)
-    b_ring(1, True)
-    halos(True)
 
     def accumulate(c, field, first):
         left, right = field[:, 0:size], field[:, size:]
@@ -326,18 +377,9 @@
             part = fields_b[p, h * (nz // 2) : (h + 1) * (nz // 2)]
             accumulate(nz + 2 * p + h, part.reshape(nz // 2 * HALF, 2 * size), False)
 
-    evaluate(done, done + 1)
-    done += 1
-    a_first(False)
-    a_ring(1, True)
-    b_ring(1, False)
-    if nz // 2 > 1:
-        b_ring(2, True)
-    evaluate(done, chunks)
-    take_a(z, True)
-
     def near_field():
         halos(False)
+        loads[2].wait()
         window[0:HALF, :] = halo[0]
         window[HALF + points :, :] = halo[1]
         q = block_ref.shape[2] // 2
@@ -366,28 +408,30 @@
 
         lax.fori_loop(0, panels, one_panel, 0)
 
-    for step in range(1, nz // 2 + 1):
-        a_ring(step, False)
-        if step < nz // 2:
-            a_ring(step + 1, True)
-            b_ring(step + 1, False)
-            if step + 2 <= nz // 2:
-                b_ring(step + 2, True)
-            else:
-                bx_ring(1, True)
-        if step == 1:
-            near_field()
+    def opened():
+        halos(True)
+        fill(16)
+
+    def arrived(step):
         take_a(z + nz - step)
         if step < nz // 2:
             take_a(z + step)
-    take_b(x)
-    for step in range(1, nx // 2 + 1):
-        bx_ring(step, False)
-        if step < nx // 2:
-            bx_ring(step + 1, True)
+        if step == 1:
+            near_field()
+        fill(16)
+
+    def crossed(step):
+        if step == 1:
+            fill(chunks * nn)
+            take_b(x)
         take_b(x + nx - step)
         if step < nx // 2:
             take_b(x + step)
+
+    run_gather(
+        gathering(fields_a, fields_b, HALF // 2, sems_ax, sems_az, sems_bz, sems_bx),
+        opened, lambda: take_a(z, True), arrived, crossed,
+    )
 
     def target(p):
         return far.at[pl.ds(pl.multiple_of(p * points, points), points), :]
@@ -425,12 +469,15 @@
     swap(nn, n, narrow_peer, lambda p: mid_h, slots_n.at[n], sems_n, False)
     full_h[pl.ds(pl.multiple_of(w * step, step), step), :] = slots_sum(slots_n, nn)
     exchange(nw, w, wide_peer, lambda p: chunk(full_h, w, step), chunk(full_h, w, step), sems_w2)
+    out_h = pltpu.make_async_copy(full_h, hess_ref, sems_io.at[3])
+    out_h.start()
     remainder = image
     for j in range(blocks):
         part = full_h[j * size : (j + 1) * size, :]
-        hess_ref[j] = part
         remainder = remainder - mm(basis_ref[j], part, ((1,), (0,)))
     rest[...] = remainder
+    out_rest = pltpu.make_async_copy(rest, rest_ref, sems_io.at[4])
+    out_rest.start()
     send_g[...] = mm(remainder * scale, remainder, ((0,), (0,)))
     gstep = size // nz
     swap(nz, z, z_peer, lambda p: chunk(send_g, p, gstep), slots_gz.at[z], sems_z, True)
@@ -446,11 +493,9 @@
     swap(nn, n, narrow_peer, lambda p: mid_g2, slots_gn.at[n], sems_gn, False)
     full_g[pl.ds(pl.multiple_of(z * gstep, gstep), gstep), :] = slots_sum(slots_gn, nn)
     exchange(nz, z, z_peer, lambda p: chunk(full_g, z, gstep), chunk(full_g, z, gstep), sems_z2)
-    factor(full_g[...], work)
-    row = lax.broadcasted_iota(jnp.int32, (size, size), 0)
-    col = lax.broadcasted_iota(jnp.int32, (size, size), 1)
-    upper_ref[...] = jnp.where(row <= col, work[:, 0:size], 0.0)
-    new_ref[...] = mm(rest[...], work[:, size:], ((1,), (1,)))
+    gram_ref[...] = full_g[...]
+    out_h.wait()
+    out_rest.wait()
 
 
 def whole_step(panel, count, points, weight, basis, jacobi, agg, block, inverse, nn, nw, nz):
@@ -460,28 +505,40 @@
     coarse = inverse.shape[1]
     vmem = pl.BlockSpec(memory_space=pltpu.VMEM)
     smem = pl.BlockSpec(memory_space=pltpu.SMEM)
+    hbm = pl.BlockSpec(memory_space=pl.ANY)
     step, gstep, nx = blocks * size // nw, size // nz, nw // nz
     chunks, cols = nz + 2 * nx, nx * HALF
     dma = lambda *c: pltpu.SemaphoreType.DMA((2, *c))
     lanes = max(nx // 2, 1)
     buf = pltpu.VMEM
+    gather_sems = (
+        dma(nx),
+        pltpu.SemaphoreType.DMA((lanes, 2, 2, nz // 2)),
+        dma(2, nz // 2),
+        pltpu.SemaphoreType.DMA((nz, 2, 2, nx // 2)),
+    )
     return pl.pallas_call(
         functools.partial(step_kernel, nn, nw, nz),
         name="step",
         out_shape=(
             jax.ShapeDtypeStruct((rows, size), f32),
-            jax.ShapeDtypeStruct((blocks, size, size), f32),
+            jax.ShapeDtypeStruct((blocks * size, size), f32),
             jax.ShapeDtypeStruct((size, size), f32),
         ),
-        in_specs=[smem] * 2 + [vmem] * 7,
-        out_specs=(vmem,) * 3,
+        in_specs=[smem] * 2 + [vmem] * 2 + [hbm] + [vmem] * 2 + [hbm] * 2,
+        out_specs=(hbm, hbm, vmem),
         scratch_shapes=[
+            buf(basis.shape, f32),
+            buf(block.shape, bf16),
+            buf(inverse.shape, f32),
             buf((8, pts), f32),
             buf((nw, 8, pts), f32),
             buf((nn, 8, pts), f32),
             buf((chunks, nx // 2, 8, pts), f32),
             buf((nn, 2, pts, pts), f32),
             buf((chunks, 3, nn * pts, cols), bf16),
+            buf((nz, nx, coarse // 2, size), f32),
+            buf((nx, nz, coarse // 2, size), f32),
             buf((nx, nz, coarse, size), f32),
             buf((nn, coarse, size), f32),
             buf((nn, coarse, size), f32),
@@ -505,12 +562,9 @@
             buf((nn, gstep, size), f32),
             buf((size, size), f32),
             buf((rows, size), f32),
-            buf((size, 2 * size), f32),
-            dma(nw), dma(nn), dma(nx), dma(2, nz // 2), dma(nn), dma(2),
-            dma(nx),
-            pltpu.SemaphoreType.DMA((lanes, 2, 2, nz // 2)),
-            dma(2, nz // 2),
-            pltpu.SemaphoreType.DMA((2, 2, 2, max(nx // 2, 1))),
+            pltpu.SemaphoreType.DMA((5,)),
+            dma(nw), dma(nn), dma(nn), dma(2),
+            *gather_sems, *gather_sems,
             dma(nn),
             dma(nw), dma(nn), dma(nw), dma(nz), dma(nx), dma(nn), dma(nz),
         ],
@@ -520,11 +574,53 @@
     )(panel, count, points, weight, basis, jacobi, agg, block, inverse)
 
 
+def finish_kernel(gram_ref, rest_hbm, hess_hbm, new_ref, hess_out, upper_ref, rest, hess, work, sems):
+    size = gram_ref.shape[0]
+    get_rest = pltpu.make_async_copy(rest_hbm, rest, sems.at[0])
+    get_hess = pltpu.make_async_copy(hess_hbm, hess, sems.at[1])
+    put_hess = pltpu.make_async_copy(hess, hess_out, sems.at[2])
+    get_rest.start()
+    get_hess.start()
+    get_hess.wait()
+    put_hess.start()
+    factor(gram_ref[...], work)
+    row = lax.broadcasted_iota(jnp.int32, (size, size), 0)
+    col = lax.broadcasted_iota(jnp.int32, (size, size), 1)
+    upper_ref[...] = jnp.where(row <= col, work[:, 0:size], 0.0)
+    get_rest.wait()
+    new_ref[...] = mm(rest[...], work[:, size:], ((1,), (1,)))
+    put_hess.wait()
+
+
+def finish(gram, rest, hess):
+    f32 = jnp.float32
+    size = gram.shape[0]
+    vmem = pl.BlockSpec(memory_space=pltpu.VMEM)
+    hbm = pl.BlockSpec(memory_space=pl.ANY)
+    return pl.pallas_call(
+        finish_kernel,
+        name="finish",
+        out_shape=(
+            jax.ShapeDtypeStruct(rest.shape, f32),
+            jax.ShapeDtypeStruct(hess.shape, f32),
+            jax.ShapeDtypeStruct(gram.shape, f32),
+        ),
+        in_specs=[vmem, hbm, hbm],
+        out_specs=(vmem, hbm, vmem),
+        scratch_shapes=[
+            pltpu.VMEM(rest.shape, f32),
+            pltpu.VMEM(hess.shape, f32),
+            pltpu.VMEM((size, 2 * size), f32),
+            pltpu.SemaphoreType.DMA((3,)),
+        ],
+    )(gram, rest, hess)
+
+
 def body(
     points, quad_weight, basis, jacobi, near_panel, near_count, near_block, agg_index, coarse_inverse, nz=NZ
 ):
     block_total, comps, point_count, rhs_count = basis.shape
-    new_flat, hessenberg, upper = whole_step(
+    rest, hess, gram = whole_step(
         near_panel,
         near_count,
         points,
@@ -538,7 +634,12 @@
         lax.axis_size("wide"),
         nz,
     )
-    return (new_flat.reshape(comps, point_count, rhs_count), hessenberg, upper)
+    new_flat, hess, upper = finish(gram, rest, hess)
+    return (
+        new_flat.reshape(comps, point_count, rhs_count),
+        hess.reshape(block_total, rhs_count, rhs_count),
+        upper,
+    )
 
 
 def solution(mesh):

time: 149 us -> 148 us (level)
  local copies, waits for them, and re-layouts: 4.71 us -> 0 us
  Pallas kernels: 144 us -> 147 us
    pallas_call x0 -> x1, Pallas kernels: none -> 15.8 us  [finish(): pl.pallas_call(finish_kernel, name='finish', out_shape=(jax.ShapeDtypeStr...]
    pallas_call x1, Pallas kernels: 144 us -> 131 us  [whole_step(): pl.pallas_call(functools.partial(step_kernel, nn, nw, nz), name='step', o...]
    unnamed x3 -> x0, local copies, waits for them, and re-layouts: 4.71 us -> none
where the time goes in v3:
time: 148 us; the launch traced here: 147 us
  Pallas kernels  147 us (99%)
    pallas_call x1, Pallas kernels, whole_step(): pl.pallas_call(functools.partial(step_kernel, nn, nw, nz), name='step', o...  131 us
    pallas_call x1, Pallas kernels, finish(): pl.pallas_call(finish_kernel, name='finish', out_shape=(jax.ShapeDtypeStr...  15.8 us

profile of v3, /device:TPU:1, one launch (start us, length us, event | category | flops | bytes accessed | tf_op | source)
XLA Modules:
  0.0 147.4 jit_solution(3530504826294370007)
XLA Ops:
  0.6 130.8 %step.1 = (f32[256,128]{1,0:T(8,128)}, f32[512,128]{1,0:T(8,128)}, f32[128,128]{1,0:T(8,128)}) custom-call(s32[8,12]{1,0:T(8,128)} %panel_ref.1, s32[8]{0:T(128)} %count_ref.1, f32[2,128]{1,0:T(2,128)} %points_ref.1, f32[1,128]{1,0:T(1,128)} %bitcast.5, f32[4,256,128]{2,1,0:T(8,128)} %bitcast.4, f32[2,128]{1,0:T(2,128)} %jacobi_ref.1, s32[2,128]{1,0:T(2,128)} %agg_ref.1, ...), custom_call_target="tpu_custom_call" | custom-call | tf_op jit(solution)/shard_map/step/pallas_call | solution.py:520
  131.4 15.8 %finish.1 = (f32[256,128]{1,0:T(8,128)}, f32[512,128]{1,0:T(8,128)}, f32[128,128]{1,0:T(8,128)}) custom-call(f32[128,128]{1,0:T(8,128)} %get-tuple-element.9.gram_ref, f32[256,128]{1,0:T(8,128)} %get-tuple-element.10.rest_hbm, f32[512,128]{1,0:T(8,128)} %get-tuple-element.11.hess_hbm), custom_call_target="tpu_custom_call" | custom-call | tf_op jit(solution)/shard_map/finish/pallas_call | solution.py:600

commit v4 on v3

--- a/solution.py
+++ b/solution.py
@@ -13,7 +13,8 @@
 HIGH = lax.Precision.HIGHEST
 MESH = pl.DeviceIdType.MESH
 NZ = 8
-PANEL = 16
+PANEL = 32
+GROUP = 8
 HALF = 64
 
 
@@ -21,48 +22,49 @@
     return lax.dot_general(a, b, (dims, ((), ())), precision=HIGH, preferred_element_type=jnp.float32)
 
 
-def swap(count, me, device, src, dst, sems, go):
+def drain(sem, ref):
+    pltpu.make_async_copy(ref, ref, sem).wait()
+
+
+def swap(count, me, device, src, dst, sems, whole, go):
+    if not go:
+        drain(sems.at[0], whole)
+        drain(sems.at[1], whole)
+        return
+
     def one(k, carry):
         peer = lax.rem(me + k, count)
-        copy = pltpu.make_async_remote_copy(
+        pltpu.make_async_remote_copy(
             src_ref=src(peer),
             dst_ref=dst,
-            send_sem=sems.at[0, k],
-            recv_sem=sems.at[1, k],
+            send_sem=sems.at[0],
+            recv_sem=sems.at[1],
             device_id=device(peer),
             device_id_type=MESH,
-        )
-        if go:
-            copy.start()
-        else:
-            copy.wait()
+        ).start()
         return carry
 
     lax.fori_loop(1, count, one, 0)
 
 
-def exchange(count, me, device, src, dst, sems):
-    swap(count, me, device, src, dst, sems, True)
-    swap(count, me, device, src, dst, sems, False)
-
-
-def ring(count, me, device, block, half, sems, step, go):
+def exchange(count, me, device, src, dst, sems, whole):
+    swap(count, me, device, src, dst, sems, whole, True)
+    swap(count, me, device, src, dst, sems, whole, False)
+
+
+def ring(count, me, device, block, half, send_sem, recv_sem, step):
     back = step - 1
     for way, peer, origin in ((0, me + 1, me + count - back), (1, me + count - 1, me + back)):
         peer, origin = lax.rem(peer, count), lax.rem(origin, count)
         ref = half(origin, way) if step == count // 2 else block(origin)
-        copy = pltpu.make_async_remote_copy(
+        pltpu.make_async_remote_copy(
             src_ref=ref,
             dst_ref=ref,
-            send_sem=sems.at[0, way, back],
-            recv_sem=sems.at[1, way, back],
+            send_sem=send_sem,
+            recv_sem=recv_sem,
             device_id=device(peer),
             device_id_type=MESH,
-        )
-        if go:
-            copy.start()
-        else:
-            copy.wait()
+        ).start()
 
 
 def slots_sum(ref, count):
@@ -72,22 +74,18 @@
     return total
 
 
-def greet(nn, nw, n, w, before, after):
+def greet(groups, others):
     barrier = pltpu.get_barrier_semaphore()
-
-    def wide_one(k, carry):
-        pl.semaphore_signal(barrier, inc=1, device_id={"wide": lax.rem(w + k, nw)}, device_id_type=MESH)
-        return carry
-
-    def narrow_one(k, carry):
-        pl.semaphore_signal(barrier, inc=1, device_id={"narrow": lax.rem(n + k, nn)}, device_id_type=MESH)
-        return carry
-
-    lax.fori_loop(1, nw, wide_one, 0)
-    lax.fori_loop(1, nn, narrow_one, 0)
-    for peer in (before, after):
+    for count, me, device in groups:
+
+        def one(k, carry):
+            pl.semaphore_signal(barrier, inc=1, device_id=device(lax.rem(me + k, count)), device_id_type=MESH)
+            return carry
+
+        lax.fori_loop(1, count, one, 0)
+    for peer in others:
         pl.semaphore_signal(barrier, inc=1, device_id=peer, device_id_type=MESH)
-    return barrier
+    return barrier, sum(count - 1 for count, _, _ in groups) + len(others)
 
 
 def factor(gram, work):
@@ -96,17 +94,35 @@
     cols = lax.broadcasted_iota(jnp.int32, (size, size), 1)
     work[:, 0:size] = gram
     work[:, size:] = (rows == cols).astype(jnp.float32)
-    sub = lax.broadcasted_iota(jnp.int32, (PANEL, 1), 0)
+    sub = lax.broadcasted_iota(jnp.int32, (PANEL, size), 0)
     for base in range(0, size, PANEL):
-        panel = work[base : base + PANEL, :]
-        for k in range(PANEL):
-            pivot = panel[k : k + 1, base + k : base + k + 1]
-            row = panel[k : k + 1, :] * lax.rsqrt(pivot)
-            left = panel[:, base + k : base + k + 1] * lax.rsqrt(pivot)
-            panel = jnp.where(sub == k, row, jnp.where(sub > k, panel - left * row, panel))
-        work[base : base + PANEL, :] = panel
+        sides = [work[base : base + PANEL, 0:size], work[base : base + PANEL, size:]]
+        for k in range(0, PANEL, GROUP):
+            lefts = [
+                jnp.broadcast_to(sides[0][:, base + k + j : base + k + j + 1], (PANEL, size)) for j in range(GROUP)
+            ]
+            tops = [[side[k + j : k + j + 1, :] for side in sides] for j in range(GROUP)]
+            for j in range(GROUP):
+                inv = lax.rsqrt(lefts[j][k + j : k + j + 1, :])
+                lefts[j] = lefts[j] * inv
+                tops[j] = [top * inv for top in tops[j]]
+                for i in range(j + 1, GROUP):
+                    share = lefts[j][k + i : k + i + 1, :]
+                    lefts[i] = lefts[i] - lefts[j] * share
+                    tops[i] = [top - share * done for top, done in zip(tops[i], tops[j])]
+            for s in range(2):
+                new = sides[s]
+                for j in range(GROUP):
+                    new = new - lefts[j] * tops[j][s]
+                new = jnp.where(sub >= k + GROUP, new, sides[s])
+                for j in range(GROUP):
+                    new = jnp.where(sub == k + j, tops[j][s], new)
+                sides[s] = new
+        work[base : base + PANEL, 0:size] = sides[0]
+        work[base : base + PANEL, size:] = sides[1]
         if base + PANEL < size:
-            below = mm(panel[:, 0:size], panel, ((0,), (0,)))
+            panel = jnp.concatenate(sides, axis=1)
+            below = mm(sides[0], panel, ((0,), (0,)))
             work[base + PANEL :, :] = work[base + PANEL :, :] - below[base + PANEL :, :]
 
 
@@ -121,13 +137,13 @@
     basis_ref, block_ref, inverse_ref,
     info, info_w, info_n, sources, columns, green,
     rhs_a, rhs_b, rhs_all, parts, part_slots, fields_a, fields_b, window, halo, far, far_slots, near,
-    send_h, slots_h, mid_h, slots_n, full_h,
+    send_h, slots_z, mid_z, slots_x, mid_h, slots_n, full_h,
     send_g, slots_gz, mid_g, slots_gx, mid_g2, slots_gn, full_g,
     rest,
-    sems_io, sems_iw, sems_in, sems_cn, sems_halo,
-    sems_cax, sems_caz, sems_cbz, sems_cbx,
-    sems_ax, sems_az, sems_bz, sems_bx, sems_far,
-    sems_w, sems_n, sems_w2, sems_z, sems_x, sems_gn, sems_z2,
+    sems_io, sems_ix, sems_iz, sems_in, sems_cn, sems_halo,
+    sems_cax, sems_cs, sems_caz, sems_cbz, sems_cbx,
+    sems_ax, sems_as, sems_az, sems_bz, sems_bx, sems_far,
+    sems_hz, sems_hx, sems_n, sems_hx2, sems_hz2, sems_z, sems_x, sems_gn, sems_z2,
 ):
     f32, bf16 = jnp.float32, jnp.bfloat16
     n = lax.axis_index("narrow")
@@ -144,7 +160,16 @@
         return {"narrow": p // nw, "wide": lax.rem(p, nw)}
 
     before, after = flat_peer(lax.rem(flat + total - 1, total)), flat_peer(lax.rem(flat + 1, total))
-    barrier = greet(nn, nw, n, w, before, after)
+    def narrow_peer(p):
+        return {"narrow": p}
+
+    def z_peer(p):
+        return {"wide": x * nz + p}
+
+    def x_peer(p):
+        return {"wide": p * nz + z}
+
+    barrier, greeted = greet(((nn, n, narrow_peer), (nx, x, x_peer), (nz, z, z_peer)), (before, after))
     loads = [
         pltpu.make_async_copy(src, dst, sems_io.at[i])
         for i, (src, dst) in enumerate(((basis_hbm, basis_ref), (inverse_hbm, inverse_ref), (block_hbm, block_ref)))
@@ -152,59 +177,64 @@
     for load in loads:
         load.start()
 
-    def wide_peer(p):
-        return {"wide": p}
-
-    def narrow_peer(p):
-        return {"narrow": p}
-
-    def z_peer(p):
-        return {"wide": x * nz + p}
-
-    def x_peer(p):
-        return {"wide": p * nz + z}
-
     lanes = max(nx // 2, 1)
 
-    def gathering(buf_a, buf_b, cut, sem_ax, sem_az, sem_bz, sem_bx):
+    def gathering(buf_a, buf_b, cut, sem_ax, sem_send, sem_az, sem_bz, sem_bx):
+        deep, cross = nz // 2, nx // 2
+
         def a_first(go):
-            swap(nx, x, x_peer, lambda p: buf_a.at[z, x], buf_a.at[z, x], sem_ax, go)
+            swap(nx, x, x_peer, lambda p: buf_a.at[z, x], buf_a.at[z, x], sem_ax, buf_a.at[0, 0 : nx - 1], go)
 
         def a_ring(j, step, go):
+            if not go:
+                drain(sem_az.at[j, step - 1], buf_a.at[0:2, 0:2] if step < deep else buf_a.at[0, 0:2])
+                return
             ring(
                 nz, z, z_peer,
                 lambda p: buf_a.at[p, 2 * j : 2 * j + 2],
                 lambda p, way: buf_a.at[p, 2 * j + way],
-                sem_az.at[j], step, go,
+                sem_send.at[0], sem_az.at[j, step - 1], step,
             )
 
         def part(ref, way):
             return ref.at[:cut] if way == 0 else ref.at[cut:]
 
         def b_ring(step, go):
+            if not go:
+                drain(sem_bz.at[step - 1], buf_b.at[0, 0:2] if step < deep else buf_b.at[0, 0])
+                return
             ring(
                 nz, z, z_peer,
                 lambda p: buf_b.at[x, p],
                 lambda p, way: part(buf_b.at[x, p], way),
-                sem_bz, step, go,
+                sem_send.at[1], sem_bz.at[step - 1], step,
             )
 
         def bx_ring(shift, step, go):
-            for at, sign in ((2 * shift - 1, -1), (2 * shift, 1)):
-                if at < 0 or at >= nz:
-                    continue
+            signs = [sign for at, sign in ((2 * shift - 1, -1), (2 * shift, 1)) if 0 <= at < nz]
+            if not go:
+                drain(sem_bx.at[shift], buf_b.at[0, 0 : len(signs) * (2 if step < cross else 1)])
+                return
+            for sign in signs:
                 q = lax.rem(z + nz + sign * shift, nz)
                 ring(
                     nx, x, x_peer,
                     lambda p: buf_b.at[p, q],
                     lambda p, way: part(buf_b.at[p, q], way),
-                    sem_bx.at[at], step, go,
+                    sem_send.at[2], sem_bx.at[shift if step == 1 else deep + 1], step,
                 )
 
-        return a_first, a_ring, b_ring, bx_ring
+        def close():
+            if cross > 1:
+                drain(sem_bx.at[deep + 1], buf_b.at[0])
+            drain(sem_send.at[0], buf_a.at[0 : nz - 1])
+            drain(sem_send.at[1], buf_b.at[0, 0 : nz - 1])
+            drain(sem_send.at[2], buf_b.at[0 : nx - 1])
+
+        return a_first, a_ring, b_ring, bx_ring, close
 
     def run_gather(steps, opened, own, arrived, crossed):
-        a_first, a_ring, b_ring, bx_ring = steps
+        a_first, a_ring, b_ring, bx_ring, close = steps
         deep, wide_steps = nz // 2, nx // 2
 
         def next_b(step):
@@ -232,22 +262,22 @@
             if step < deep:
                 next_b(step + 1)
             next_x(step)
+            if step == deep:
+                crossed(1)
             for j in range(lanes):
                 a_ring(j, step, False)
                 if step < deep:
                     a_ring(j, step + 1, True)
             arrived(step)
-        crossed(1)
+        close()
         if wide_steps > 1:
-            for shift in range(deep + 1):
-                bx_ring(shift, 2, False)
             crossed(2)
 
     info[...] = jnp.zeros_like(info)
     info[0:2, :] = points_ref[...]
     info[2:3, :] = ELASTIC * weight_ref[...]
     info_n[n] = info[...]
-    info_w[w] = info[...]
+    info_w[z, x] = info[...]
 
     ids = lax.broadcasted_iota(jnp.int32, (coarse, points), 0)
     member = [(ids == agg_ref[a : a + 1, :]).astype(f32) for a in range(2)]
@@ -256,26 +286,30 @@
     rhs = mm(member[0], newest[0], ((1,), (0,))) + mm(member[1], newest[1], ((1,), (0,)))
     rhs_a[z, x] = rhs[0 : coarse // 2, :]
     rhs_b[x, z] = rhs[coarse // 2 :, :]
-    pl.semaphore_wait(barrier, nw + nn)
-    swap(nn, n, narrow_peer, lambda p: info, info_n.at[n], sems_in, True)
-    swap(nw, w, wide_peer, lambda p: info, info_w.at[w], sems_iw, True)
+    pl.semaphore_wait(barrier, greeted)
+    swap(nx, x, x_peer, lambda p: info, info_w.at[z, x], sems_ix, info_w.at[0, 0 : nx - 1], True)
+    swap(nn, n, narrow_peer, lambda p: info, info_n.at[n], sems_in, info_n.at[0 : nn - 1], True)
     chunks = nz + 2 * nx
     tall = 32
     pairs = nx // 2
 
+    def spread_info():
+        swap(nx, x, x_peer, lambda p: info, info_w.at[z, x], sems_ix, info_w.at[0, 0 : nx - 1], False)
+        swap(nz, z, z_peer, lambda p: info_w.at[z], info_w.at[z], sems_iz, info_w.at[0 : nz - 1], True)
+
     def prepare():
-        swap(nn, n, narrow_peer, lambda p: info, info_n.at[n], sems_in, False)
-        swap(nw, w, wide_peer, lambda p: info, info_w.at[w], sems_iw, False)
+        swap(nn, n, narrow_peer, lambda p: info, info_n.at[n], sems_in, info_n.at[0 : nn - 1], False)
+        swap(nz, z, z_peer, lambda p: info_w.at[z], info_w.at[z], sems_iz, info_w.at[0 : nz - 1], False)
         lane = lax.broadcasted_iota(jnp.int32, (8, points), 1)
         for p in range(nz):
             for m in range(pairs):
-                one, two = info_w[(2 * m) * nz + p], info_w[(2 * m + 1) * nz + p]
+                one, two = info_w[p, 2 * m], info_w[p, 2 * m + 1]
                 sources[p, m] = jnp.where(lane < HALF, one, pltpu.roll(two, HALF, 1))
         for p in range(nx):
             for h in range(2):
                 for m in range(pairs):
-                    at = p * nz + h * (nz // 2) + 2 * m
-                    one, two = info_w[at], info_w[at + 1]
+                    at = h * (nz // 2) + 2 * m
+                    one, two = info_w[at, p], info_w[at + 1, p]
                     sources[nz + 2 * p + h, m] = jnp.where(lane < HALF, pltpu.roll(one, HALF, 1), two)
         for t in range(nn):
             tile = info_n[t]
@@ -312,8 +346,8 @@
         done[0] = last
 
     run_gather(
-        gathering(rhs_a, rhs_b, 16, sems_cax, sems_caz, sems_cbz, sems_cbx),
-        lambda: None, prepare, lambda step: fill(16), lambda step: None,
+        gathering(rhs_a, rhs_b, 16, sems_cax, sems_cs, sems_caz, sems_cbz, sems_cbx),
+        spread_info, prepare, lambda step: fill(16), lambda step: None,
     )
     for p in range(nx):
         for q in range(nz):
@@ -323,10 +357,10 @@
 
     inverse = inverse_ref[...].reshape(nn * coarse, nw * coarse)
     parts[...] = mm(inverse, rhs_all[...].reshape(nw * coarse, size), ((1,), (0,))).reshape(nn, coarse, size)
-    swap(nn, n, narrow_peer, lambda p: parts.at[p], part_slots.at[n], sems_cn, True)
+    swap(nn, n, narrow_peer, lambda p: parts.at[p], part_slots.at[n], sems_cn, part_slots.at[0 : nn - 1], True)
     part_slots[n] = parts[n]
     fill(32)
-    swap(nn, n, narrow_peer, lambda p: parts.at[p], part_slots.at[n], sems_cn, False)
+    swap(nn, n, narrow_peer, lambda p: parts.at[p], part_slots.at[n], sems_cn, part_slots.at[0 : nn - 1], False)
     sol = slots_sum(part_slots, nn)
     for a in range(2):
         lifted = mm(member[a], sol, ((0,), (0,)))
@@ -422,23 +456,23 @@
 
     def crossed(step):
         if step == 1:
-            fill(chunks * nn)
+            fill(128)
             take_b(x)
         take_b(x + nx - step)
         if step < nx // 2:
             take_b(x + step)
 
     run_gather(
-        gathering(fields_a, fields_b, HALF // 2, sems_ax, sems_az, sems_bz, sems_bx),
+        gathering(fields_a, fields_b, HALF // 2, sems_ax, sems_as, sems_az, sems_bz, sems_bx),
         opened, lambda: take_a(z, True), arrived, crossed,
     )
 
     def target(p):
         return far.at[pl.ds(pl.multiple_of(p * points, points), points), :]
 
-    swap(nn, n, narrow_peer, target, far_slots.at[n], sems_far, True)
+    swap(nn, n, narrow_peer, target, far_slots.at[n], sems_far, far_slots.at[0 : nn - 1], True)
     far_slots[n] = far[pl.ds(pl.multiple_of(n * points, points), points), :]
-    swap(nn, n, narrow_peer, target, far_slots.at[n], sems_far, False)
+    swap(nn, n, narrow_peer, target, far_slots.at[n], sems_far, far_slots.at[0 : nn - 1], False)
     far_sum = slots_sum(far_slots, nn)
     image = jnp.concatenate(
         [
@@ -455,20 +489,29 @@
     weighted = image * scale
     for j in range(blocks):
         send_h[j * size : (j + 1) * size, :] = mm(basis_ref[j], weighted, ((0,), (0,)))
-    step = blocks * size // nw
-
     def chunk(ref, p, rows):
         return ref.at[pl.ds(pl.multiple_of(p * rows, rows), rows), :]
 
-    swap(nw, w, wide_peer, lambda p: chunk(send_h, p, step), slots_h.at[w], sems_w, True)
-    slots_h[w] = send_h[pl.ds(pl.multiple_of(w * step, step), step), :]
-    swap(nw, w, wide_peer, lambda p: chunk(send_h, p, step), slots_h.at[w], sems_w, False)
-    mid_h[...] = slots_sum(slots_h, nw)
-    swap(nn, n, narrow_peer, lambda p: mid_h, slots_n.at[n], sems_n, True)
-    slots_n[n] = mid_h[...]
-    swap(nn, n, narrow_peer, lambda p: mid_h, slots_n.at[n], sems_n, False)
-    full_h[pl.ds(pl.multiple_of(w * step, step), step), :] = slots_sum(slots_n, nn)
-    exchange(nw, w, wide_peer, lambda p: chunk(full_h, w, step), chunk(full_h, w, step), sems_w2)
+    def first(ref, count, rows):
+        return ref.at[0 : (count - 1) * rows, :]
+
+    def reduce(count, me, device, src, slots, sems):
+        piece = slots.shape[1]
+        whole = slots.at[0 : count - 1]
+        pick = (lambda p: chunk(src, p, piece)) if src.shape[0] > piece else (lambda p: src)
+        swap(count, me, device, pick, slots.at[me], sems, whole, True)
+        slots[me] = pick(me)[...]
+        swap(count, me, device, pick, slots.at[me], sems, whole, False)
+        return slots_sum(slots, count)
+
+    tall_step, step = blocks * size // nz, blocks * size // nw
+    mid_z[...] = reduce(nz, z, z_peer, send_h, slots_z, sems_hz)
+    mid_h[...] = reduce(nx, x, x_peer, mid_z, slots_x, sems_hx)
+    block_z = chunk(full_h, z, tall_step)
+    block_z[pl.ds(pl.multiple_of(x * step, step), step), :] = reduce(nn, n, narrow_peer, mid_h, slots_n, sems_n)
+    mine = full_h.at[pl.ds(pl.multiple_of(z * tall_step + x * step, step), step), :]
+    exchange(nx, x, x_peer, lambda p: mine, mine, sems_hx2, first(full_h, nx, step))
+    exchange(nz, z, z_peer, lambda p: block_z, block_z, sems_hz2, first(full_h, nz, tall_step))
     out_h = pltpu.make_async_copy(full_h, hess_ref, sems_io.at[3])
     out_h.start()
     remainder = image
@@ -480,19 +523,10 @@
     out_rest.start()
     send_g[...] = mm(remainder * scale, remainder, ((0,), (0,)))
     gstep = size // nz
-    swap(nz, z, z_peer, lambda p: chunk(send_g, p, gstep), slots_gz.at[z], sems_z, True)
-    slots_gz[z] = send_g[pl.ds(pl.multiple_of(z * gstep, gstep), gstep), :]
-    swap(nz, z, z_peer, lambda p: chunk(send_g, p, gstep), slots_gz.at[z], sems_z, False)
-    mid_g[...] = slots_sum(slots_gz, nz)
-    swap(nx, x, x_peer, lambda p: mid_g, slots_gx.at[x], sems_x, True)
-    slots_gx[x] = mid_g[...]
-    swap(nx, x, x_peer, lambda p: mid_g, slots_gx.at[x], sems_x, False)
-    mid_g2[...] = slots_sum(slots_gx, nx)
-    swap(nn, n, narrow_peer, lambda p: mid_g2, slots_gn.at[n], sems_gn, True)
-    slots_gn[n] = mid_g2[...]
-    swap(nn, n, narrow_peer, lambda p: mid_g2, slots_gn.at[n], sems_gn, False)
-    full_g[pl.ds(pl.multiple_of(z * gstep, gstep), gstep), :] = slots_sum(slots_gn, nn)
-    exchange(nz, z, z_peer, lambda p: chunk(full_g, z, gstep), chunk(full_g, z, gstep), sems_z2)
+    mid_g[...] = reduce(nz, z, z_peer, send_g, slots_gz, sems_z)
+    mid_g2[...] = reduce(nx, x, x_peer, mid_g, slots_gx, sems_x)
+    full_g[pl.ds(pl.multiple_of(z * gstep, gstep), gstep), :] = reduce(nn, n, narrow_peer, mid_g2, slots_gn, sems_gn)
+    exchange(nz, z, z_peer, lambda p: chunk(full_g, z, gstep), chunk(full_g, z, gstep), sems_z2, first(full_g, nz, gstep))
     gram_ref[...] = full_g[...]
     out_h.wait()
     out_rest.wait()
@@ -508,15 +542,10 @@
     hbm = pl.BlockSpec(memory_space=pl.ANY)
     step, gstep, nx = blocks * size // nw, size // nz, nw // nz
     chunks, cols = nz + 2 * nx, nx * HALF
-    dma = lambda *c: pltpu.SemaphoreType.DMA((2, *c))
+    dma = lambda *c: pltpu.SemaphoreType.DMA(c)
     lanes = max(nx // 2, 1)
     buf = pltpu.VMEM
-    gather_sems = (
-        dma(nx),
-        pltpu.SemaphoreType.DMA((lanes, 2, 2, nz // 2)),
-        dma(2, nz // 2),
-        pltpu.SemaphoreType.DMA((nz, 2, 2, nx // 2)),
-    )
+    gather_sems = (dma(2), dma(3), dma(lanes, nz // 2), dma(nz // 2), dma(nz // 2 + 2))
     return pl.pallas_call(
         functools.partial(step_kernel, nn, nw, nz),
         name="step",
@@ -532,7 +561,7 @@
             buf(block.shape, bf16),
             buf(inverse.shape, f32),
             buf((8, pts), f32),
-            buf((nw, 8, pts), f32),
+            buf((nz, nx, 8, pts), f32),
             buf((nn, 8, pts), f32),
             buf((chunks, nx // 2, 8, pts), f32),
             buf((nn, 2, pts, pts), f32),
@@ -550,7 +579,9 @@
             buf((nn, pts, 2 * size), f32),
             buf((rows, size), f32),
             buf((blocks * size, size), f32),
-            buf((nw, step, size), f32),
+            buf((nz, nx * step, size), f32),
+            buf((nx * step, size), f32),
+            buf((nx, step, size), f32),
             buf((step, size), f32),
             buf((nn, step, size), f32),
             buf((blocks * size, size), f32),
@@ -563,10 +594,9 @@
             buf((size, size), f32),
             buf((rows, size), f32),
             pltpu.SemaphoreType.DMA((5,)),
-            dma(nw), dma(nn), dma(nn), dma(2),
+            *([dma(2)] * 4), dma(2, 2),
             *gather_sems, *gather_sems,
-            dma(nn),
-            dma(nw), dma(nn), dma(nw), dma(nz), dma(nx), dma(nn), dma(nz),
+            *([dma(2)] * 10),
         ],
         compiler_params=pltpu.CompilerParams(
             collective_id=0, has_side_effects=True, vmem_limit_bytes=60 * 1024 * 1024

time: 148 us -> 138 us (0.932)
  Pallas kernels: 147 us -> 138 us
    pallas_call x1, Pallas kernels: 15.8 us -> 6.8 us  [finish(): pl.pallas_call(finish_kernel, name='finish', out_shape=(jax.ShapeDtypeStr...]
where the time goes in v4:
time: 138 us
  Pallas kernels  138 us (100%)
    pallas_call x1, Pallas kernels, whole_step(): pl.pallas_call(functools.partial(step_kernel, nn, nw, nz), name='step', o...  131 us
    pallas_call x1, Pallas kernels, finish(): pl.pallas_call(finish_kernel, name='finish', out_shape=(jax.ShapeDtypeStr...  6.8 us

profile of v4, /device:TPU:1, one launch (start us, length us, event | category | flops | bytes accessed | tf_op | source)
XLA Modules:
  0.0 138.1 jit_solution(14787822562297295783)
XLA Ops:
  0.6 130.7 %step.1 = (f32[256,128]{1,0:T(8,128)}, f32[512,128]{1,0:T(8,128)}, f32[128,128]{1,0:T(8,128)}) custom-call(s32[8,12]{1,0:T(8,128)} %panel_ref.1, s32[8]{0:T(128)} %count_ref.1, f32[2,128]{1,0:T(2,128)} %points_ref.1, f32[1,128]{1,0:T(1,128)} %bitcast.5, f32[4,256,128]{2,1,0:T(8,128)} %bitcast.4, f32[2,128]{1,0:T(2,128)} %jacobi_ref.1, s32[2,128]{1,0:T(2,128)} %agg_ref.1, ...), custom_call_target="tpu_custom_call" | custom-call | tf_op jit(solution)/shard_map/step/pallas_call | solution.py:549
  131.3 6.8 %finish.1 = (f32[256,128]{1,0:T(8,128)}, f32[512,128]{1,0:T(8,128)}, f32[128,128]{1,0:T(8,128)}) custom-call(f32[128,128]{1,0:T(8,128)} %get-tuple-element.9.gram_ref, f32[256,128]{1,0:T(8,128)} %get-tuple-element.10.rest_hbm, f32[512,128]{1,0:T(8,128)} %get-tuple-element.11.hess_hbm), custom_call_target="tpu_custom_call" | custom-call | tf_op jit(solution)/shard_map/finish/pallas_call | solution.py:630

commit v5 on v4

--- a/solution.py
+++ b/solution.py
@@ -137,13 +137,13 @@
     basis_ref, block_ref, inverse_ref,
     info, info_w, info_n, sources, columns, green,
     rhs_a, rhs_b, rhs_all, parts, part_slots, fields_a, fields_b, window, halo, far, far_slots, near,
-    send_h, slots_z, mid_z, slots_x, mid_h, slots_n, full_h,
-    send_g, slots_gz, mid_g, slots_gx, mid_g2, slots_gn, full_g,
+    send_h, slots_n, mid_n, slots_x, mid_h, slots_z, full_h,
+    send_g, slots_gn, mid_g, slots_gx, mid_g2, slots_gz, full_g,
     rest,
     sems_io, sems_ix, sems_iz, sems_in, sems_cn, sems_halo,
     sems_cax, sems_cs, sems_caz, sems_cbz, sems_cbx,
     sems_ax, sems_as, sems_az, sems_bz, sems_bx, sems_far,
-    sems_hz, sems_hx, sems_n, sems_hx2, sems_hz2, sems_z, sems_x, sems_gn, sems_z2,
+    sems_n, sems_hx, sems_hz, sems_hx2, sems_n2, sems_gn, sems_x, sems_z, sems_gn2,
 ):
     f32, bf16 = jnp.float32, jnp.bfloat16
     n = lax.axis_index("narrow")
@@ -258,17 +258,24 @@
         next_b(1)
         next_x(0)
         own()
+        if deep > 1:
+            next_b(2)
         for step in range(1, deep + 1):
-            if step < deep:
-                next_b(step + 1)
-            next_x(step)
-            if step == deep:
-                crossed(1)
             for j in range(lanes):
                 a_ring(j, step, False)
                 if step < deep:
                     a_ring(j, step + 1, True)
+            if step + 2 <= deep:
+                next_b(step + 2)
+            if step < deep:
+                next_x(step)
+            if step == deep - 1:
+                next_x(deep)
             arrived(step)
+            if step == max(1, deep - 2):
+                crossed(0)
+            if step == deep - 1:
+                crossed(1)
         close()
         if wide_steps > 1:
             crossed(2)
@@ -347,7 +354,7 @@
 
     run_gather(
         gathering(rhs_a, rhs_b, 16, sems_cax, sems_cs, sems_caz, sems_cbz, sems_cbx),
-        spread_info, prepare, lambda step: fill(16), lambda step: None,
+        spread_info, prepare, lambda step: fill(20), lambda step: None,
     )
     for p in range(nx):
         for q in range(nz):
@@ -359,7 +366,7 @@
     parts[...] = mm(inverse, rhs_all[...].reshape(nw * coarse, size), ((1,), (0,))).reshape(nn, coarse, size)
     swap(nn, n, narrow_peer, lambda p: parts.at[p], part_slots.at[n], sems_cn, part_slots.at[0 : nn - 1], True)
     part_slots[n] = parts[n]
-    fill(32)
+    fill(36)
     swap(nn, n, narrow_peer, lambda p: parts.at[p], part_slots.at[n], sems_cn, part_slots.at[0 : nn - 1], False)
     sol = slots_sum(part_slots, nn)
     for a in range(2):
@@ -444,20 +451,20 @@
 
     def opened():
         halos(True)
-        fill(16)
+        fill(12)
 
     def arrived(step):
+        fill(128)
         take_a(z + nz - step)
         if step < nz // 2:
             take_a(z + step)
         if step == 1:
             near_field()
-        fill(16)
 
     def crossed(step):
-        if step == 1:
-            fill(128)
+        if step == 0:
             take_b(x)
+            return
         take_b(x + nx - step)
         if step < nx // 2:
             take_b(x + step)
@@ -504,14 +511,14 @@
         swap(count, me, device, pick, slots.at[me], sems, whole, False)
         return slots_sum(slots, count)
 
-    tall_step, step = blocks * size // nz, blocks * size // nw
-    mid_z[...] = reduce(nz, z, z_peer, send_h, slots_z, sems_hz)
-    mid_h[...] = reduce(nx, x, x_peer, mid_z, slots_x, sems_hx)
-    block_z = chunk(full_h, z, tall_step)
-    block_z[pl.ds(pl.multiple_of(x * step, step), step), :] = reduce(nn, n, narrow_peer, mid_h, slots_n, sems_n)
-    mine = full_h.at[pl.ds(pl.multiple_of(z * tall_step + x * step, step), step), :]
-    exchange(nx, x, x_peer, lambda p: mine, mine, sems_hx2, first(full_h, nx, step))
-    exchange(nz, z, z_peer, lambda p: block_z, block_z, sems_hz2, first(full_h, nz, tall_step))
+    wide_piece, piece = blocks * size // nn, blocks * size // nn // nx
+    mid_n[...] = reduce(nn, n, narrow_peer, send_h, slots_n, sems_n)
+    mid_h[...] = reduce(nx, x, x_peer, mid_n, slots_x, sems_hx)
+    mine = full_h.at[pl.ds(pl.multiple_of(n * wide_piece + x * piece, piece), piece), :]
+    mine[...] = reduce(nz, z, z_peer, mid_h, slots_z, sems_hz)
+    exchange(nx, x, x_peer, lambda p: mine, mine, sems_hx2, first(full_h, nx, piece))
+    block_n = chunk(full_h, n, wide_piece)
+    exchange(nn, n, narrow_peer, lambda p: block_n, block_n, sems_n2, first(full_h, nn, wide_piece))
     out_h = pltpu.make_async_copy(full_h, hess_ref, sems_io.at[3])
     out_h.start()
     remainder = image
@@ -522,11 +529,12 @@
     out_rest = pltpu.make_async_copy(rest, rest_ref, sems_io.at[4])
     out_rest.start()
     send_g[...] = mm(remainder * scale, remainder, ((0,), (0,)))
-    gstep = size // nz
-    mid_g[...] = reduce(nz, z, z_peer, send_g, slots_gz, sems_z)
+    gstep = size // nn
+    mid_g[...] = reduce(nn, n, narrow_peer, send_g, slots_gn, sems_gn)
     mid_g2[...] = reduce(nx, x, x_peer, mid_g, slots_gx, sems_x)
-    full_g[pl.ds(pl.multiple_of(z * gstep, gstep), gstep), :] = reduce(nn, n, narrow_peer, mid_g2, slots_gn, sems_gn)
-    exchange(nz, z, z_peer, lambda p: chunk(full_g, z, gstep), chunk(full_g, z, gstep), sems_z2, first(full_g, nz, gstep))
+    own_g = chunk(full_g, n, gstep)
+    own_g[...] = reduce(nz, z, z_peer, mid_g2, slots_gz, sems_z)
+    exchange(nn, n, narrow_peer, lambda p: own_g, own_g, sems_gn2, first(full_g, nn, gstep))
     gram_ref[...] = full_g[...]
     out_h.wait()
     out_rest.wait()
@@ -540,7 +548,8 @@
     vmem = pl.BlockSpec(memory_space=pltpu.VMEM)
     smem = pl.BlockSpec(memory_space=pltpu.SMEM)
     hbm = pl.BlockSpec(memory_space=pl.ANY)
-    step, gstep, nx = blocks * size // nw, size // nz, nw // nz
+    nx = nw // nz
+    step, gstep = blocks * size // nn // nx, size // nn
     chunks, cols = nz + 2 * nx, nx * HALF
     dma = lambda *c: pltpu.SemaphoreType.DMA(c)
     lanes = max(nx // 2, 1)
@@ -579,18 +588,18 @@
             buf((nn, pts, 2 * size), f32),
             buf((rows, size), f32),
             buf((blocks * size, size), f32),
-            buf((nz, nx * step, size), f32),
+            buf((nn, nx * step, size), f32),
             buf((nx * step, size), f32),
             buf((nx, step, size), f32),
             buf((step, size), f32),
-            buf((nn, step, size), f32),
+            buf((nz, step, size), f32),
             buf((blocks * size, size), f32),
             buf((size, size), f32),
-            buf((nz, gstep, size), f32),
+            buf((nn, gstep, size), f32),
             buf((gstep, size), f32),
             buf((nx, gstep, size), f32),
             buf((gstep, size), f32),
-            buf((nn, gstep, size), f32),
+            buf((nz, gstep, size), f32),
             buf((size, size), f32),
             buf((rows, size), f32),
             pltpu.SemaphoreType.DMA((5,)),

time: 138 us -> 132 us (0.957)
  Pallas kernels: 138 us -> 131 us
    pallas_call x1, Pallas kernels: 131 us -> 124 us  [whole_step(): pl.pallas_call(functools.partial(step_kernel, nn, nw, nz), name='step', o...]
where the time goes in v5:
time: 132 us
  Pallas kernels  131 us (99%)
    pallas_call x1, Pallas kernels, whole_step(): pl.pallas_call(functools.partial(step_kernel, nn, nw, nz), name='step', o...  124 us
    pallas_call x1, Pallas kernels, finish(): pl.pallas_call(finish_kernel, name='finish', out_shape=(jax.ShapeDtypeStr...  6.8 us

profile of v5, /device:TPU:1, one launch (start us, length us, event | category | flops | bytes accessed | tf_op | source)
XLA Modules:
  0.0 131.9 jit_solution(5318695029287586541)
XLA Ops:
  0.6 124.4 %step.1 = (f32[256,128]{1,0:T(8,128)}, f32[512,128]{1,0:T(8,128)}, f32[128,128]{1,0:T(8,128)}) custom-call(s32[8,12]{1,0:T(8,128)} %panel_ref.1, s32[8]{0:T(128)} %count_ref.1, f32[2,128]{1,0:T(2,128)} %points_ref.1, f32[1,128]{1,0:T(1,128)} %bitcast.5, f32[4,256,128]{2,1,0:T(8,128)} %bitcast.4, f32[2,128]{1,0:T(2,128)} %jacobi_ref.1, s32[2,128]{1,0:T(2,128)} %agg_ref.1, ...), custom_call_target="tpu_custom_call" | custom-call | tf_op jit(solution)/shard_map/step/pallas_call | solution.py:558
  125.1 6.8 %finish.1 = (f32[256,128]{1,0:T(8,128)}, f32[512,128]{1,0:T(8,128)}, f32[128,128]{1,0:T(8,128)}) custom-call(f32[128,128]{1,0:T(8,128)} %get-tuple-element.9.gram_ref, f32[256,128]{1,0:T(8,128)} %get-tuple-element.10.rest_hbm, f32[512,128]{1,0:T(8,128)} %get-tuple-element.11.hess_hbm), custom_call_target="tpu_custom_call" | custom-call | tf_op jit(solution)/shard_map/finish/pallas_call | solution.py:639

commit v6 on v5

--- a/solution.py
+++ b/solution.py
@@ -14,7 +14,7 @@
 MESH = pl.DeviceIdType.MESH
 NZ = 8
 PANEL = 32
-GROUP = 8
+GROUP = 16
 HALF = 64
 
 
@@ -390,23 +390,51 @@
         halo_copy(0, fields_b.at[x, z], after, go)
         halo_copy(1, fields_a.at[z, x], before, go)
 
+    def accumulate_rows(c, field, first, i):
+        left, right = field[:, 0:size], field[:, size:]
+        rows = pl.ds(pl.multiple_of(i * 2 * points, 2 * points), 2 * points)
+        cross = jnp.dot(green[c, 1, rows, :], field, preferred_element_type=f32)
+        one = jnp.dot(green[c, 0, rows, :], left, preferred_element_type=f32) + cross[:, size:]
+        two = jnp.dot(green[c, 2, rows, :], right, preferred_element_type=f32) + cross[:, 0:size]
+        if first:
+            far[rows, 0:size] = one
+            far[rows, size:] = two
+        else:
+            far[rows, 0:size] = far[rows, 0:size] + one
+            far[rows, size:] = far[rows, size:] + two
+
     def accumulate(c, field, first):
-        left, right = field[:, 0:size], field[:, size:]
-
         def rows_of(i, carry):
-            rows = pl.ds(pl.multiple_of(i * 2 * points, 2 * points), 2 * points)
-            cross = jnp.dot(green[c, 1, rows, :], field, preferred_element_type=f32)
-            one = jnp.dot(green[c, 0, rows, :], left, preferred_element_type=f32) + cross[:, size:]
-            two = jnp.dot(green[c, 2, rows, :], right, preferred_element_type=f32) + cross[:, 0:size]
-            if first:
-                far[rows, 0:size] = one
-                far[rows, size:] = two
+            accumulate_rows(c, field, first, i)
+            return carry
+
+        lax.fori_loop(0, nn // 2, rows_of, 0)
+
+    def send_far(p):
+        pltpu.make_async_remote_copy(
+            src_ref=far.at[pl.ds(pl.multiple_of(p * points, points), points), :],
+            dst_ref=far_slots.at[n],
+            send_sem=sems_far.at[0],
+            recv_sem=sems_far.at[1],
+            device_id=narrow_peer(p),
+            device_id_type=MESH,
+        ).start()
+
+    def part_b(p, h):
+        return fields_b[p, h * (nz // 2) : (h + 1) * (nz // 2)].reshape(nz // 2 * HALF, 2 * size)
+
+    def finish_far(p):
+        p = lax.rem(p, nx)
+        pairs_of = nn // 2
+        for shift in sorted(range(pairs_of), key=lambda k: -min(k, pairs_of - k)):
+            i = lax.rem(n // 2 + shift, pairs_of)
+            for h in range(2):
+                accumulate_rows(nz + 2 * p + h, part_b(p, h), False, i)
+            if shift:
+                send_far(2 * i)
+                send_far(2 * i + 1)
             else:
-                far[rows, 0:size] = far[rows, 0:size] + one
-                far[rows, size:] = far[rows, size:] + two
-            return carry
-
-        lax.fori_loop(0, nn // 2, rows_of, 0)
+                send_far(2 * i + 1 - lax.rem(n, 2))
 
     def take_a(p, first=False):
         p = lax.rem(p, nz)
@@ -465,6 +493,9 @@
         if step == 0:
             take_b(x)
             return
+        if step == 2:
+            finish_far(x + nx - step)
+            return
         take_b(x + nx - step)
         if step < nx // 2:
             take_b(x + step)
@@ -474,22 +505,16 @@
         opened, lambda: take_a(z, True), arrived, crossed,
     )
 
-    def target(p):
-        return far.at[pl.ds(pl.multiple_of(p * points, points), points), :]
-
-    swap(nn, n, narrow_peer, target, far_slots.at[n], sems_far, far_slots.at[0 : nn - 1], True)
+    if nx == 2:
+        for shift in range(1, nn):
+            send_far(lax.rem(n + shift, nn))
     far_slots[n] = far[pl.ds(pl.multiple_of(n * points, points), points), :]
-    swap(nn, n, narrow_peer, target, far_slots.at[n], sems_far, far_slots.at[0 : nn - 1], False)
-    far_sum = slots_sum(far_slots, nn)
-    image = jnp.concatenate(
-        [
-            0.5 * window[HALF : HALF + points, a * size : (a + 1) * size].astype(f32)
-            + far_sum[:, a * size : (a + 1) * size]
-            + near[a * points : (a + 1) * points, :]
-            for a in range(2)
-        ],
-        axis=0,
-    )
+    base = jnp.concatenate([near[0:points, :], near[points:, :]], axis=1)
+    base = base + 0.5 * window[HALF : HALF + points, :].astype(f32)
+    drain(sems_far.at[0], far_slots.at[0 : nn - 1])
+    drain(sems_far.at[1], far_slots.at[0 : nn - 1])
+    base = base + slots_sum(far_slots, nn)
+    image = jnp.concatenate([base[:, 0:size], base[:, size:]], axis=0)
 
     spread = column(weight_ref[...], points)
     scale = jnp.concatenate([spread, spread], axis=0)

time: 132 us -> 130 us (0.985)
  Pallas kernels: 131 us -> 129 us
    pallas_call x1, Pallas kernels: 124 us -> 123 us  [whole_step(): pl.pallas_call(functools.partial(step_kernel, nn, nw, nz), name='step', o...]
where the time goes in v6:
time: 130 us
  Pallas kernels  129 us (99%)
    pallas_call x1, Pallas kernels, whole_step(): pl.pallas_call(functools.partial(step_kernel, nn, nw, nz), name='step', o...  123 us
    pallas_call x1, Pallas kernels, finish(): pl.pallas_call(finish_kernel, name='finish', out_shape=(jax.ShapeDtypeStr...  6.35 us

profile of v6, /device:TPU:1, one launch (start us, length us, event | category | flops | bytes accessed | tf_op | source)
XLA Modules:
  0.0 129.8 jit_solution(6289356818010974373)
XLA Ops:
  0.6 122.7 %step.1 = (f32[256,128]{1,0:T(8,128)}, f32[512,128]{1,0:T(8,128)}, f32[128,128]{1,0:T(8,128)}) custom-call(s32[8,12]{1,0:T(8,128)} %panel_ref.1, s32[8]{0:T(128)} %count_ref.1, f32[2,128]{1,0:T(2,128)} %points_ref.1, f32[1,128]{1,0:T(1,128)} %bitcast.5, f32[4,256,128]{2,1,0:T(8,128)} %bitcast.4, f32[2,128]{1,0:T(2,128)} %jacobi_ref.1, s32[2,128]{1,0:T(2,128)} %agg_ref.1, ...), custom_call_target="tpu_custom_call" | custom-call | tf_op jit(solution)/shard_map/step/pallas_call | solution.py:583
  123.3 6.4 %finish.1 = (f32[256,128]{1,0:T(8,128)}, f32[512,128]{1,0:T(8,128)}, f32[128,128]{1,0:T(8,128)}) custom-call(f32[128,128]{1,0:T(8,128)} %get-tuple-element.9.gram_ref, f32[256,128]{1,0:T(8,128)} %get-tuple-element.10.rest_hbm, f32[512,128]{1,0:T(8,128)} %get-tuple-element.11.hess_hbm), custom_call_target="tpu_custom_call" | custom-call | tf_op jit(solution)/shard_map/finish/pallas_call | solution.py:664

commit v7 on v6

--- a/solution.py
+++ b/solution.py
@@ -352,9 +352,14 @@
         evaluate(done[0], last)
         done[0] = last
 
+    def rhs_arrived(step):
+        if step == 1:
+            prepare()
+        fill(20)
+
     run_gather(
         gathering(rhs_a, rhs_b, 16, sems_cax, sems_cs, sems_caz, sems_cbz, sems_cbx),
-        spread_info, prepare, lambda step: fill(20), lambda step: None,
+        spread_info, lambda: None, rhs_arrived, lambda step: None,
     )
     for p in range(nx):
         for q in range(nz):

time: 130 us -> 130 us (level)
  no operation moved by 1% of the time
where the time goes in v7:
time: 130 us
  Pallas kernels  129 us (99%)
    pallas_call x1, Pallas kernels, whole_step(): pl.pallas_call(functools.partial(step_kernel, nn, nw, nz), name='step', o...  123 us
    pallas_call x1, Pallas kernels, finish(): pl.pallas_call(finish_kernel, name='finish', out_shape=(jax.ShapeDtypeStr...  6.35 us

profile of v7, /device:TPU:1, one launch (start us, length us, event | category | flops | bytes accessed | tf_op | source)
XLA Modules:
  0.0 129.9 jit_solution(5011570726073199250)
XLA Ops:
  0.6 122.7 %step.1 = (f32[256,128]{1,0:T(8,128)}, f32[512,128]{1,0:T(8,128)}, f32[128,128]{1,0:T(8,128)}) custom-call(s32[8,12]{1,0:T(8,128)} %panel_ref.1, s32[8]{0:T(128)} %count_ref.1, f32[2,128]{1,0:T(2,128)} %points_ref.1, f32[1,128]{1,0:T(1,128)} %bitcast.5, f32[4,256,128]{2,1,0:T(8,128)} %bitcast.4, f32[2,128]{1,0:T(2,128)} %jacobi_ref.1, s32[2,128]{1,0:T(2,128)} %agg_ref.1, ...), custom_call_target="tpu_custom_call" | custom-call | tf_op jit(solution)/shard_map/step/pallas_call | solution.py:588
  123.3 6.3 %finish.1 = (f32[256,128]{1,0:T(8,128)}, f32[512,128]{1,0:T(8,128)}, f32[128,128]{1,0:T(8,128)}) custom-call(f32[128,128]{1,0:T(8,128)} %get-tuple-element.9.gram_ref, f32[256,128]{1,0:T(8,128)} %get-tuple-element.10.rest_hbm, f32[512,128]{1,0:T(8,128)} %get-tuple-element.11.hess_hbm), custom_call_target="tpu_custom_call" | custom-call | tf_op jit(solution)/shard_map/finish/pallas_call | solution.py:669
